TPU v7x, 32 devices: a whole 2x2x4 slice. The times are simulated.
32 devices in a mesh: gx: 4 (over z), gy: 8 (over y, x, core).
Axes of the slice: x: 2, y: 2, z: 4, core: 2. Of those that a mesh axis runs over, the one named last changes fastest.
Arguments:
- velocity: float32 [128, 256, 3, 256], P('gx', 'gy'), may hold values from -6 to 6
- fiber_loads: float32 [3, 49152], P(None, ('gx', 'gy')), may hold values from -96 to 96
- fractions: float32 [3, 49152], P(None, ('gx', 'gy')), may hold values from 0 to 1
- corners: int32 [3, 49152], P(None, ('gx', 'gy')), may hold values from 0 to 255, as said below
- neighbours: int32 [49152], P(('gx', 'gy')), may hold values from 0 to 1535
- counts: int32 [1024], P(('gx', 'gy')), may hold values from 1 to 48, as said below
Outputs:
- velocity_next: float32 [128, 256, 3, 256], P('gx', 'gy')
- fiber_velocity: float32 [3, 49152], P(None, ('gx', 'gy'))
Inputs may be any that keep to these rules, and one draw needn't show every extreme that they name: `counts`: in every draw some destination device receives 48 live slots from every source device. For a slot whose destination device has x block a and y block b: corners[0] is a * 32 + o mod 128 with o from -2 to 30, corners[1] is b * 32 + o mod 256 with o from -2 to 30, corners[2] any cell along z.
All inputs are finite; a program needn't handle non-finite values.
Results may differ from a plain program's by a relative error of at most 0.0029.
Values may be sent and summed in bfloat16 or wider, within the bound.
No kernel may reach another device: no remote copies, remote signals or barrier semaphores. Data moves between devices by JAX's collectives and lax.ppermute only.
A program may use at most 128 MiB of HBM per device.

v0:
```python
import jax
import jax.numpy as jnp
from jax import lax
from jax.sharding import PartitionSpec as P

viscosity = 0.15


def padded_2(value, sides, width):
    for axis, dim in sides:
        peers, length = (lax.axis_size(axis), value.shape[dim])
        up = [(i, (i + 1) % peers) for i in range(peers)]
        down = [(j, i) for i, j in up]
        last = lax.slice_in_dim(value, length - width, length, axis=dim)
        first = lax.slice_in_dim(value, 0, width, axis=dim)
        before = lax.ppermute(last, axis, up)
        after = lax.ppermute(first, axis, down)
        value = jnp.concatenate([before, value, after], axis=dim)
    return value


def peskin(fraction):
    nodes = jnp.arange(4, dtype=jnp.float32).reshape((4,) + (1,) * fraction.ndim)
    return 0.25 * (1.0 + jnp.cos(0.5 * jnp.pi * (1.0 + fraction[None] - nodes)))


def tables(block_data, pad_x, pad_y, cells_z):
    fraction = block_data[3:6]
    corner = block_data[6:9].astype(jnp.int32)
    weight_x = peskin(fraction[0])
    weight_y = peskin(fraction[1])
    weight_z = peskin(fraction[2])
    columns_x = jnp.arange(pad_x, dtype=jnp.int32)[None, :]
    columns_y = jnp.arange(pad_y, dtype=jnp.int32)[None, :]
    columns_z = jnp.arange(cells_z, dtype=jnp.int32)[None, :]
    along_x = jnp.zeros((block_data.shape[1], pad_x), jnp.float32)
    along_y = jnp.zeros((block_data.shape[1], pad_y), jnp.float32)
    depth_wts = jnp.zeros((block_data.shape[1], cells_z), jnp.float32)
    for offset in range(4):
        along_x = along_x + weight_x[offset][:, None] * (columns_x == (corner[0] + offset)[:, None])
        along_y = along_y + weight_y[offset][:, None] * (columns_y == (corner[1] + offset)[:, None])
        depth_wts = depth_wts + weight_z[offset][:, None] * (
            columns_z == ((corner[2] + offset) % cells_z)[:, None]
        )
    plane_wts = (along_x[:, :, None] * along_y[:, None, :]).reshape(
        block_data.shape[1], pad_x * pad_y
    )
    return (plane_wts.astype(jnp.bfloat16), depth_wts)


def laplace_of(padded):
    center = padded[1:-1, 1:-1]
    result = padded[2:, 1:-1] + padded[:-2, 1:-1]
    result = result + padded[1:-1, 2:] + padded[1:-1, :-2]
    result = result + jnp.roll(center, -1, 3) + jnp.roll(center, 1, 3)
    return center + viscosity * (result - 6.0 * center)


def body(velocity, fiber_loads, fractions, corners, neighbours, counts):
    groups_x = lax.axis_size("gx")
    groups_y = lax.axis_size("gy")
    devices = groups_x * groups_y
    slot_count = fiber_loads.shape[1]
    per_peer = slot_count // devices
    cells_x, cells_y, cells_z = (velocity.shape[0], velocity.shape[1], velocity.shape[3])
    pad_x = cells_x + 4
    pad_y = cells_y + 4
    whole_x = cells_x * groups_x
    whole_y = cells_y * groups_y
    live_mask = (
        (jnp.arange(per_peer, dtype=jnp.int32)[None, :] < counts[:, None])
        .reshape(-1)
        .astype(jnp.float32)
    )
    position = corners.astype(jnp.float32) + fractions
    partner = jnp.take(position, neighbours, axis=1)
    stiffness = jnp.array([2.0 / whole_x, 2.0 / whole_y, 2.0 / cells_z], jnp.float32)[:, None]
    forcing = (fiber_loads + stiffness * (partner - position)) * live_mask
    bucket = jnp.arange(slot_count, dtype=jnp.int32) // per_peer
    local_x = (corners[0] - bucket // groups_y * cells_x + 2) % whole_x
    local_y = (corners[1] - bucket % groups_y * cells_y + 2) % whole_y
    local_corner = jnp.stack([local_x, local_y, corners[2]]).astype(jnp.float32)
    payload = jnp.concatenate([forcing, fractions, local_corner], 0)
    received = lax.all_to_all(payload, ("gx", "gy"), split_axis=1, concat_axis=1, tiled=True)
    block_len = per_peer * groups_y

    def spread_block(block_idx, running):
        block_data = lax.dynamic_slice_in_dim(received, block_idx * block_len, block_len, 1)
        plane_wts, depth_wts = tables(block_data, pad_x, pad_y, cells_z)
        push_rows = (block_data[0:3].T[:, :, None] * depth_wts[:, None, :]).reshape(
            block_len, 3 * cells_z
        )
        return running + jnp.einsum(
            "pa,pb->ab",
            plane_wts,
            push_rows.astype(jnp.bfloat16),
            preferred_element_type=jnp.float32,
        )

    grid_sum = lax.fori_loop(
        0, groups_x, spread_block, jnp.zeros((pad_x * pad_y, 3 * cells_z), jnp.float32)
    )
    grid_sum = grid_sum.reshape(pad_x, pad_y, 3, cells_z)
    ghosts = padded_2(grid_sum, (("gx", 0), ("gy", 1)), 2)
    folded = ghosts[4 : cells_x + 4]
    folded = folded.at[:2].add(ghosts[:2]).at[-2:].add(ghosts[cells_x + 6 :])
    inner = folded[:, 4 : cells_y + 4]
    inner = inner.at[:, :2].add(folded[:, :2]).at[:, -2:].add(folded[:, cells_y + 6 :])
    field = velocity + inner
    for sweep in range(2):
        padded = padded_2(field, (("gx", 0), ("gy", 1)), 1)
        field = laplace_of(padded)
    rounded = padded_2(field.astype(jnp.bfloat16), (("gx", 0), ("gy", 1)), 2)
    flat_vel = rounded.reshape(pad_x * pad_y, 3 * cells_z)

    def gather_block(block_idx, result):
        block_data = lax.dynamic_slice_in_dim(received, block_idx * block_len, block_len, 1)
        plane_wts, depth_wts = tables(block_data, pad_x, pad_y, cells_z)
        mixed_rows = jnp.dot(plane_wts, flat_vel, preferred_element_type=jnp.float32).reshape(
            block_len, 3, cells_z
        )
        values = jnp.sum(mixed_rows * depth_wts[:, None, :], axis=2)
        return lax.dynamic_update_slice_in_dim(result, values.T, block_idx * block_len, 1)

    sampled = lax.fori_loop(0, groups_x, gather_block, jnp.zeros((3, slot_count), jnp.float32))
    returned = lax.all_to_all(sampled, ("gx", "gy"), split_axis=1, concat_axis=1, tiled=True)
    return (field, returned * live_mask)


def solution(mesh):
    return jax.shard_map(
        body,
        mesh=mesh,
        in_specs=(
            P("gx", "gy", None, None),
            P(None, ("gx", "gy")),
            P(None, ("gx", "gy")),
            P(None, ("gx", "gy")),
            P(("gx", "gy")),
            P(("gx", "gy")),
        ),
        out_specs=(P("gx", "gy", None, None), P(None, ("gx", "gy"))),
        check_vma=False,
    )
```

profile of v0, /device:TPU:0, one launch (start us, length us, event | category | flops | bytes accessed | tf_op | source)
XLA Modules:
  0.0 220.0 jit_solution(1982585952467728534)
XLA Ops:
  4.1 2.6 %gather_fusion = f32[1536,3]{1,0:T(8,128)S(1)} fusion(f32[3,1536]{0,1:T(8,128)S(1)} %copy.91, s32[2048]{0:T(1024)S(1)} %pad_clamp_fusion), kind=kCustom, calls=%fused_computation | custom fusion | bytes 43008 | tf_op jit(solution)/shard_map/jit(_take)/gather | solution.py:76
  10.4 7.3 %all-to-all-start = ((f32[32,1,432]{2,1,0:T(1,128)}), f32[32,1,432]{2,1,0:T(1,128)S(1)}, u32[]{:S(2)}, u32[]{:S(2)}) async-start(f32[32,1,432]{2,1,0:T(1,128)} %reshape.1713), calls=%async_computation | async-start | bytes 131072 | tf_op jit(solution)/shard_map/all_to_all | solution.py:84
  17.8 7.4 %all-to-all-done = f32[32,1,432]{2,1,0:T(1,128)S(1)} async-done(((f32[32,1,432]{2,1,0:T(1,128)}), f32[32,1,432]{2,1,0:T(1,128)S(1)}, u32[]{:S(2)}, u32[]{:S(2)}) %all-to-all-start) | async-done | bytes 55328 | tf_op jit(solution)/shard_map/all_to_all | solution.py:84
  26.8 24.6 %while.36 = (s32[]{:T(128)}, f32[1296,768]{1,0:T(8,128)}, f32[9,1536]{1,0:T(8,128)S(1)}, s32[]{:T(128)}, s32[]{:T(128)}, /*index=5*/s32[]{}, s32[]{:T(128)}, s32[]{:T(128)}, s32[]{}, s32[]{}, /*index=10*/s32[]{}) while((s32[]{:T(128)}, f32[1296,768]{1,0:T(8,128)}, f32[9,1536]{1,0:T(8,128)S(1)}, s32[]{:T(128)}, s32[]{:T(128)}, ...), condition=%wide.region_1.2_spmd.clone, body=%wide.region_0.1_spmd.clone.sunk | while | flops 769414272 | bytes 14289645 | solution.py:100
  28.2 3.2 %convolution_add_fusion.2 = f32[1296,768]{1,0:T(8,128)} fusion(bf16[384,1296]{0,1:T(8,128)(2,1)S(1)} %convert_element_type.197, bf16[384,768]{0,1:T(8,128)(2,1)S(1)} %bitcast.51, f32[1296,768]{1,0:T(8,128)} %get-tuple-element.581, pred[]{:T(512)S(6)} %compare.50), kind=kOutput, calls=%fused_computation.67.clone.1 | convolution fusion | flops 766402560 | bytes 9547777 | tf_op jit(solution)/shard_map/while/body/eval_jaxpr/pa,pb->ab/dot_general | solution.py:93
  32.7 5.3 %convolution_add_fusion.2 = f32[1296,768]{1,0:T(8,128)} fusion(bf16[384,1296]{0,1:T(8,128)(2,1)S(1)} %convert_element_type.197, bf16[384,768]{0,1:T(8,128)(2,1)S(1)} %bitcast.51, f32[1296,768]{1,0:T(8,128)} %get-tuple-element.581, pred[]{:T(512)S(6)} %compare.50), kind=kOutput, calls=%fused_computation.67.clone.1 | convolution fusion | flops 766402560 | bytes 9547777 | tf_op jit(solution)/shard_map/while/body/eval_jaxpr/pa,pb->ab/dot_general | solution.py:93
  39.4 5.3 %convolution_add_fusion.2 = f32[1296,768]{1,0:T(8,128)} fusion(bf16[384,1296]{0,1:T(8,128)(2,1)S(1)} %convert_element_type.197, bf16[384,768]{0,1:T(8,128)(2,1)S(1)} %bitcast.51, f32[1296,768]{1,0:T(8,128)} %get-tuple-element.581, pred[]{:T(512)S(6)} %compare.50), kind=kOutput, calls=%fused_computation.67.clone.1 | convolution fusion | flops 766402560 | bytes 9547777 | tf_op jit(solution)/shard_map/while/body/eval_jaxpr/pa,pb->ab/dot_general | solution.py:93
  46.1 5.3 %convolution_add_fusion.2 = f32[1296,768]{1,0:T(8,128)} fusion(bf16[384,1296]{0,1:T(8,128)(2,1)S(1)} %convert_element_type.197, bf16[384,768]{0,1:T(8,128)(2,1)S(1)} %bitcast.51, f32[1296,768]{1,0:T(8,128)} %get-tuple-element.581, pred[]{:T(512)S(6)} %compare.50), kind=kOutput, calls=%fused_computation.67.clone.1 | convolution fusion | flops 766402560 | bytes 9547777 | tf_op jit(solution)/shard_map/while/body/eval_jaxpr/pa,pb->ab/dot_general | solution.py:93
  53.2 7.4 %reshape.1663 = f32[36,36,3,256]{3,2,1,0:T(4,128)} reshape(f32[1296,768]{1,0:T(8,128)} %get-tuple-element.250) | data formatting | bytes 7962624 | tf_op jit(solution)/shard_map/reshape | solution.py:103
  60.7 3.3 %collective-permute-start.1 = (f32[2,36,3,256]{3,2,1,0:T(4,128)S(1)}, f32[2,36,3,256]{3,2,1,0:T(4,128)S(1)}, u32[]{:S(2)}, u32[]{:S(2)}) collective-permute-start(f32[2,36,3,256]{3,2,1,0:T(4,128)S(1)} %slice.685), channel_id=1, source_target_pairs={{8,0},{16,8},{24,16},{0,24},{9,1},{17,9},{25,17},{1,25},{10,2},{18... | collective-permute-start | bytes 663560 | tf_op jit(solution)/shard_map/ppermute | solution.py:17
  64.1 3.8 %constant_dynamic-update-slice_fusion.1 = f32[40,36,3,256]{3,2,1,0:T(4,128)S(1)} fusion(f32[40,36,3,256]{3,2,1,0:T(4,128)S(1)} %constant_dynamic-update-slice_fusion.2, f32[36,36,3,256]{3,2,1,0:T(4,128)} %reshape.1663), kind=kLoop, calls=%fused_computation.218 | loop fusion | bytes 9289728
  67.8 2.4 %collective-permute-done.1 = f32[2,36,3,256]{3,2,1,0:T(4,128)S(1)} collective-permute-done((f32[2,36,3,256]{3,2,1,0:T(4,128)S(1)}, f32[2,36,3,256]{3,2,1,0:T(4,128)S(1)}, u32[]{:S(2)}, u32[]{:S(2)}) %collective-permute-start.1) | collective-permute-done | bytes 221216 | tf_op jit(solution)/shard_map/ppermute | solution.py:17
  70.4 2.5 %copy-done = f32[40,36,3,256]{3,2,1,0:T(4,128)} copy-done((f32[40,36,3,256]{3,2,1,0:T(4,128)}, f32[40,36,3,256]{3,2,1,0:T(4,128)S(1)}, u32[]{:S(2)}) %copy-start) | copy-done | bytes 4423704
  73.1 2.6 %collective-permute-start.3 = (f32[40,2,3,256]{3,2,1,0:T(4,128)S(1)}, f32[40,2,3,256]{3,2,1,0:T(4,128)S(1)}, u32[]{:S(2)}, u32[]{:S(2)}) collective-permute-start(f32[40,2,3,256]{3,2,1,0:T(4,128)S(1)} %get-tuple-element.375), channel_id=1, source_target_pairs={{1,0},{2,1},{3,2},{4,3},{5,4},{6,5},{7,6},{0,7},{9,8},{10,9},{11,1... | collective-permute-start | bytes 737288 | tf_op jit(solution)/shard_map/ppermute | solution.py:17
  75.7 8.3 %collective-permute-done.2 = f32[40,2,3,256]{3,2,1,0:T(4,128)S(1)} collective-permute-done((f32[40,2,3,256]{3,2,1,0:T(4,128)S(1)}, f32[40,2,3,256]{3,2,1,0:T(4,128)S(1)}, u32[]{:S(2)}, u32[]{:S(2)}) %collective-permute-start.2) | collective-permute-done | bytes 245792 | tf_op jit(solution)/shard_map/ppermute | solution.py:16
  83.9 7.3 %pad_maximum_fusion = f32[40,40,3,256]{3,2,1,0:T(4,128)} fusion(f32[40,2,3,256]{3,2,1,0:T(4,128)S(1)} %collective-permute-done.3, f32[40,36,3,256]{3,2,1,0:T(4,128)} %copy-done, f32[40,2,3,256]{3,2,1,0:T(4,128)S(1)} %collective-permute-done.2), kind=kLoop, calls=%fused_computation.133 | loop fusion | flops 2457600 | bytes 9830400 | tf_op jit(solution)/shard_map/concatenate | solution.py:18
  91.2 3.5 %slice.780 = f32[32,40,3,256]{3,2,1,0:T(4,128)S(1)} slice(f32[40,40,3,256]{3,2,1,0:T(4,128)} %pad_maximum_fusion), slice={[4:36], [0:40], [0:3], [0:256]} | slice | bytes 7864320 | tf_op jit(solution)/shard_map/slice | solution.py:105
  97.9 3.0 %copy_add_fusion = f32[32,32,3,256]{3,2,1,0:T(4,128)S(1)} fusion(f32[32,32,3,256]{3,2,1,0:T(4,128)S(1)} %fusion.33, f32[32,32,3,256]{3,1,2,0:T(8,128)S(1)} %copy-done.4), kind=kLoop, calls=%fused_computation.166 | loop fusion | flops 786432 | bytes 9437184 | tf_op jit(solution)/shard_map/add | solution.py:109
  101.0 4.3 %collective-permute-start.4 = (f32[1,32,3,256]{3,2,1,0:T(4,128)S(1)}, f32[1,32,3,256]{3,2,1,0:T(4,128)S(1)}, u32[]{:S(2)}, u32[]{:S(2)}) collective-permute-start(f32[1,32,3,256]{3,2,1,0:T(4,128)S(1)} %get-tuple-element.391), channel_id=1, source_target_pairs={{8,0},{16,8},{24,16},{0,24},{9,1},{17,9},{25,17},{1,25},{10,2},{18... | collective-permute-start | bytes 294920 | tf_op jit(solution)/shard_map/ppermute | solution.py:17
  105.3 5.2 %fusion.50 = (f32[32,32,3,255]{3,2,1,0:T(4,128)S(1)}, f32[32,32,3,255]{3,2,1,0:T(4,128)}) fusion(f32[32,32,3,256]{3,2,1,0:T(4,128)S(1)} %copy_add_fusion), kind=kLoop, calls=%fused_computation.226 | loop fusion | bytes 12533760 | tf_op jit(solution)/shard_map/jit(_roll_static)/slice | solution.py:55
  110.5 1.5 collective-permute-done.5
  112.7 1.5 fusion.49
  114.2 1.9 collective-permute-done.6
  116.1 1.8 collective-permute-done.7
  117.9 16.6 %fusion.28 = f32[32,32,3,256]{3,2,1,0:T(4,128)S(1)} fusion(f32[32,32,3,256]{3,2,1,0:T(4,128)S(1)} %copy_add_fusion, f32[34,1,3,256]{3,2,1,0:T(4,128)S(1)} %collective-permute-done.7, f32[1,32,3,256]{3,2,1,0:T(4,128)S(1)} %collective-permute-done.4, f32[1,32,3,256]{3,2,1,0:T(4,128)S(1)} %collective-permute-done.5, ...), kind=kLoop, calls=%fused_computation.156 | loop fusion | flops 14942208 | bytes 12988416 | tf_op jit(solution)/shard_map/add | solution.py:56
  134.5 2.3 %collective-permute-start.8 = (f32[1,32,3,256]{3,2,1,0:T(4,128)S(1)}, f32[1,32,3,256]{3,2,1,0:T(4,128)S(1)}, u32[]{:S(2)}, u32[]{:S(2)}) collective-permute-start(f32[1,32,3,256]{3,2,1,0:T(4,128)S(1)} %get-tuple-element.381), channel_id=1, source_target_pairs={{8,0},{16,8},{24,16},{0,24},{9,1},{17,9},{25,17},{1,25},{10,2},{18... | collective-permute-start | bytes 294920 | tf_op jit(solution)/shard_map/ppermute | solution.py:17
  136.8 4.8 %fusion.47 = (f32[32,32,3,255]{3,2,1,0:T(4,128)S(1)}, f32[32,32,3,255]{3,2,1,0:T(4,128)}) fusion(f32[32,32,3,256]{3,2,1,0:T(4,128)S(1)} %fusion.28), kind=kLoop, calls=%fused_computation.223 | loop fusion | bytes 12533760 | tf_op jit(solution)/shard_map/jit(_roll_static)/slice | solution.py:55
  141.6 2.0 collective-permute-done.9
  143.6 1.2 collective-permute-start.10
  144.8 1.5 fusion.48
  146.3 1.5 collective-permute-done.10
  147.8 2.4 %collective-permute-done.11 = f32[34,1,3,256]{3,2,1,0:T(4,128)S(1)} collective-permute-done((f32[34,1,3,256]{3,2,1,0:T(4,128)S(1)}, f32[34,1,3,256]{3,2,1,0:T(4,128)S(1)}, u32[]{:S(2)}, u32[]{:S(2)}) %collective-permute-start.11) | collective-permute-done | bytes 104480 | tf_op jit(solution)/shard_map/ppermute | solution.py:16
  150.2 17.5 %fusion.43 = (bf16[32,32,3,256]{3,2,1,0:T(4,128)(2,1)S(1)}, f32[32,32,3,256]{3,2,1,0:T(4,128)}) fusion(f32[32,32,3,256]{3,2,1,0:T(4,128)S(1)} %fusion.28, f32[32,32,3,255]{3,2,1,0:T(4,128)S(1)} %copy-done.2, f32[32,32,3,1]{3,2,1,0:T(4,128)S(1)} %get-tuple-element.385, f32[32,32,3,1]{3,2,1,0:T(4,128)S(1)} %get-tuple-element.384, ...), kind=kLoop, calls=%fused_computation.220 | loop fusion | flops 15728640 | bytes 14561280 | tf_op jit(solution)/shard_map/convert_element_type | solution.py:113
  167.8 1.3 collective-permute-start.12
  169.1 2.6 %collective-permute-start.13 = (bf16[2,32,3,256]{3,2,1,0:T(4,128)(2,1)S(1)}, bf16[2,32,3,256]{3,2,1,0:T(4,128)(2,1)S(1)}, u32[]{:S(2)}, u32[]{:S(2)}) collective-permute-start(bf16[2,32,3,256]{3,2,1,0:T(4,128)(2,1)S(1)} %get-tuple-element.397), channel_id=1, source_target_pairs={{8,0},{16,8},{24,16},{0,24},{9,1},{17,9},{25,17},{1,25},{10,2},{18... | collective-permute-start | bytes 294920 | tf_op jit(solution)/shard_map/ppermute | solution.py:17
  171.6 3.0 %collective-permute-done.12 = bf16[2,32,3,256]{3,2,1,0:T(4,128)(2,1)S(1)} collective-permute-done((bf16[2,32,3,256]{3,2,1,0:T(4,128)(2,1)S(1)}, bf16[2,32,3,256]{3,2,1,0:T(4,128)(2,1)S(1)}, u32[]{:S(2)}, u32[]{:S(2)}) %collective-permute-start.12) | collective-permute-done | bytes 98336 | tf_op jit(solution)/shard_map/ppermute | solution.py:16
  175.7 2.6 %collective-permute-start.15 = (bf16[36,2,3,256]{3,2,1,0:T(4,128)(2,1)S(1)}, bf16[36,2,3,256]{3,2,1,0:T(4,128)(2,1)S(1)}, u32[]{:S(2)}, u32[]{:S(2)}) collective-permute-start(bf16[36,2,3,256]{3,2,1,0:T(4,128)(2,1)S(1)} %get-tuple-element.395), channel_id=1, source_target_pairs={{1,0},{2,1},{3,2},{4,3},{5,4},{6,5},{7,6},{0,7},{9,8},{10,9},{11,1... | collective-permute-start | bytes 331784 | tf_op jit(solution)/shard_map/ppermute | solution.py:17
  178.4 3.0 %collective-permute-done.14 = bf16[36,2,3,256]{3,2,1,0:T(4,128)(2,1)S(1)} collective-permute-done((bf16[36,2,3,256]{3,2,1,0:T(4,128)(2,1)S(1)}, bf16[36,2,3,256]{3,2,1,0:T(4,128)(2,1)S(1)}, u32[]{:S(2)}, u32[]{:S(2)}) %collective-permute-start.14) | collective-permute-done | bytes 110624 | tf_op jit(solution)/shard_map/ppermute | solution.py:16
  181.4 3.7 %pad_maximum_fusion.17 = bf16[36,36,3,256]{3,2,1,0:T(4,128)(2,1)S(1)} fusion(bf16[36,2,3,256]{3,2,1,0:T(4,128)(2,1)S(1)} %collective-permute-done.15, bf16[2,32,3,256]{3,2,1,0:T(4,128)(2,1)S(1)} %collective-permute-done.13, bf16[32,32,3,256]{3,2,1,0:T(4,128)(2,1)S(1)} %get-tuple-element.340, bf16[2,32,3,256]{3,2,1,0:T(4,128)(2,1)S(1)} %collective-permute-done.12, ...), kind=kLoop, calls=%fused_computation.167 | loop fusion | flops 3981312 | bytes 3981312 | tf_op jit(solution)/shard_map/concatenate | solution.py:18
  185.7 2.4 %copy.96 = bf16[1296,768]{0,1:T(8,128)(2,1)} copy(bf16[1296,768]{1,0:T(8,128)(2,1)S(1)} %bitcast.53) | data formatting | bytes 3981312 | tf_op jit(solution)/shard_map/while | solution.py:125
  188.1 17.1 %while.35 = (s32[]{:T(128)}, f32[3,1536]{1,0:T(4,128)S(1)}, f32[9,1536]{1,0:T(8,128)S(1)}, bf16[1296,768]{0,1:T(8,128)(2,1)}, s32[]{:T(128)}, /*index=5*/s32[]{:...) while((s32[]{:T(128)}, f32[3,1536]{1,0:T(4,128)S(1)}, f32[9,1536]{1,0:T(8,128)S(1)}, ...), condition=%wide.region_4.5_spmd, body=%wide.region_2.4_spmd.sunk | while | flops 767422464 | bytes 7141103 | solution.py:125
  189.3 3.0 %fusion.68 = f32[384,3]{0,1:T(4,128)S(1)} fusion(bf16[384,1296,1]{0,1,2:T(8,128)(2,1)S(1)} %reshape.1718, bf16[3,256,1296]{2,1,0:T(8,128)(2,1)} %bitcast.54, f32[384,256]{0,1:T(8,128)S(1)} %select_add_fusion.14), kind=kOutput, calls=%fused_computation.3.clone.1 | convolution fusion | flops 765000576 | bytes 3383808 | tf_op jit(solution)/shard_map/while/body/eval_jaxpr/dot_general | solution.py:119
  193.6 3.0 %fusion.68 = f32[384,3]{0,1:T(4,128)S(1)} fusion(bf16[384,1296,1]{0,1,2:T(8,128)(2,1)S(1)} %reshape.1718, bf16[3,256,1296]{2,1,0:T(8,128)(2,1)} %bitcast.54, f32[384,256]{0,1:T(8,128)S(1)} %select_add_fusion.14), kind=kOutput, calls=%fused_computation.3.clone.1 | convolution fusion | flops 765000576 | bytes 3383808 | tf_op jit(solution)/shard_map/while/body/eval_jaxpr/dot_general | solution.py:119
  197.9 3.0 %fusion.68 = f32[384,3]{0,1:T(4,128)S(1)} fusion(bf16[384,1296,1]{0,1,2:T(8,128)(2,1)S(1)} %reshape.1718, bf16[3,256,1296]{2,1,0:T(8,128)(2,1)} %bitcast.54, f32[384,256]{0,1:T(8,128)S(1)} %select_add_fusion.14), kind=kOutput, calls=%fused_computation.3.clone.1 | convolution fusion | flops 765000576 | bytes 3383808 | tf_op jit(solution)/shard_map/while/body/eval_jaxpr/dot_general | solution.py:119
  202.1 3.0 %fusion.68 = f32[384,3]{0,1:T(4,128)S(1)} fusion(bf16[384,1296,1]{0,1,2:T(8,128)(2,1)S(1)} %reshape.1718, bf16[3,256,1296]{2,1,0:T(8,128)(2,1)} %bitcast.54, f32[384,256]{0,1:T(8,128)S(1)} %select_add_fusion.14), kind=kOutput, calls=%fused_computation.3.clone.1 | convolution fusion | flops 765000576 | bytes 3383808 | tf_op jit(solution)/shard_map/while/body/eval_jaxpr/dot_general | solution.py:119
  206.0 5.2 %all-to-all-start.1 = ((f32[32,1,144]{2,1,0:T(1,128)}), f32[32,1,144]{2,1,0:T(1,128)S(1)}, u32[]{:S(2)}, u32[]{:S(2)}) async-start(f32[32,1,144]{2,1,0:T(1,128)} %reshape.1715), calls=%async_computation.1 | async-start | bytes 65536 | tf_op jit(solution)/shard_map/all_to_all | solution.py:126
  211.2 4.4 %copy.99 = f32[32,32,3,256]{3,1,2,0:T(8,128)} copy(f32[32,32,3,256]{3,2,1,0:T(4,128)} %get-tuple-element.341) | data formatting | bytes 6291456
  215.6 2.8 %all-to-all-done.1 = f32[32,1,144]{2,1,0:T(1,128)S(1)} async-done(((f32[32,1,144]{2,1,0:T(1,128)}), f32[32,1,144]{2,1,0:T(1,128)S(1)}, u32[]{:S(2)}, u32[]{:S(2)}) %all-to-all-start.1) | async-done | bytes 18464 | tf_op jit(solution)/shard_map/all_to_all | solution.py:126
  (199 shorter events, 29.0 us)
Async XLA Ops:
  10.4 14.7 %all-to-all-start = ((f32[32,1,432]{2,1,0:T(1,128)}), f32[32,1,432]{2,1,0:T(1,128)S(1)}, u32[]{:S(2)}, u32[]{:S(2)}) async-start(f32[32,1,432]{2,1,0:T(1,128)} %reshape.1713), calls=%async_computation | async-start | bytes 131072 | tf_op jit(solution)/shard_map/all_to_all | solution.py:84
  52.6 11.4 %collective-permute-start = (f32[2,36,3,256]{3,2,1,0:T(4,128)S(1)}, f32[2,36,3,256]{3,2,1,0:T(4,128)S(1)}, u32[]{:S(2)}, u32[]{:S(2)}) collective-permute-start(f32[2,36,3,256]{3,2,1,0:T(4,128)S(1)} %slice.683), channel_id=1, source_target_pairs={{0,8},{8,16},{16,24},{24,0},{1,9},{9,17},{17,25},{25,1},{2,10},{10... | collective-permute-start | bytes 663560 | tf_op jit(solution)/shard_map/ppermute | solution.py:16
  60.7 9.5 %collective-permute-start.1 = (f32[2,36,3,256]{3,2,1,0:T(4,128)S(1)}, f32[2,36,3,256]{3,2,1,0:T(4,128)S(1)}, u32[]{:S(2)}, u32[]{:S(2)}) collective-permute-start(f32[2,36,3,256]{3,2,1,0:T(4,128)S(1)} %slice.685), channel_id=1, source_target_pairs={{8,0},{16,8},{24,16},{0,24},{9,1},{17,9},{25,17},{1,25},{10,2},{18... | collective-permute-start | bytes 663560 | tf_op jit(solution)/shard_map/ppermute | solution.py:17
  70.3 2.5 %copy-start = (f32[40,36,3,256]{3,2,1,0:T(4,128)}, f32[40,36,3,256]{3,2,1,0:T(4,128)S(1)}, u32[]{:S(2)}) copy-start(f32[40,36,3,256]{3,2,1,0:T(4,128)S(1)} %constant_dynamic-update-slice_fusion) | copy-start | bytes 13271044
  73.0 10.9 %collective-permute-start.2 = (f32[40,2,3,256]{3,2,1,0:T(4,128)S(1)}, f32[40,2,3,256]{3,2,1,0:T(4,128)S(1)}, u32[]{:S(2)}, u32[]{:S(2)}) collective-permute-start(f32[40,2,3,256]{3,2,1,0:T(4,128)S(1)} %get-tuple-element.374), channel_id=1, source_target_pairs={{0,1},{1,2},{2,3},{3,4},{4,5},{5,6},{6,7},{7,0},{8,9},{9,10},{10,1... | collective-permute-start | bytes 737288 | tf_op jit(solution)/shard_map/ppermute | solution.py:16
  73.1 10.9 %collective-permute-start.3 = (f32[40,2,3,256]{3,2,1,0:T(4,128)S(1)}, f32[40,2,3,256]{3,2,1,0:T(4,128)S(1)}, u32[]{:S(2)}, u32[]{:S(2)}) collective-permute-start(f32[40,2,3,256]{3,2,1,0:T(4,128)S(1)} %get-tuple-element.375), channel_id=1, source_target_pairs={{1,0},{2,1},{3,2},{4,3},{5,4},{6,5},{7,6},{0,7},{9,8},{10,9},{11,1... | collective-permute-start | bytes 737288 | tf_op jit(solution)/shard_map/ppermute | solution.py:17
  91.2 4.2 %copy-start.1 = (f32[40,36,3,256]{3,2,1,0:T(4,128)S(1)}, f32[40,36,3,256]{3,2,1,0:T(4,128)}, u32[]{:S(2)}) copy-start(f32[40,36,3,256]{3,2,1,0:T(4,128)} %copy-done) | copy-start | bytes 13271044
  96.0 1.9 copy-start.4
  101.0 9.6 %collective-permute-start.4 = (f32[1,32,3,256]{3,2,1,0:T(4,128)S(1)}, f32[1,32,3,256]{3,2,1,0:T(4,128)S(1)}, u32[]{:S(2)}, u32[]{:S(2)}) collective-permute-start(f32[1,32,3,256]{3,2,1,0:T(4,128)S(1)} %get-tuple-element.391), channel_id=1, source_target_pairs={{8,0},{16,8},{24,16},{0,24},{9,1},{17,9},{25,17},{1,25},{10,2},{18... | collective-permute-start | bytes 294920 | tf_op jit(solution)/shard_map/ppermute | solution.py:17
  105.3 6.8 %collective-permute-start.5 = (f32[1,32,3,256]{3,2,1,0:T(4,128)S(1)}, f32[1,32,3,256]{3,2,1,0:T(4,128)S(1)}, u32[]{:S(2)}, u32[]{:S(2)}) collective-permute-start(f32[1,32,3,256]{3,2,1,0:T(4,128)S(1)} %get-tuple-element.390), channel_id=1, source_target_pairs={{0,8},{8,16},{16,24},{24,0},{1,9},{9,17},{17,25},{25,1},{2,10},{10... | collective-permute-start | bytes 294920 | tf_op jit(solution)/shard_map/ppermute | solution.py:16
  112.1 3.9 %collective-permute-start.6 = (f32[34,1,3,256]{3,2,1,0:T(4,128)S(1)}, f32[34,1,3,256]{3,2,1,0:T(4,128)S(1)}, u32[]{:S(2)}, u32[]{:S(2)}) collective-permute-start(f32[34,1,3,256]{3,2,1,0:T(4,128)S(1)} %get-tuple-element.378), channel_id=1, source_target_pairs={{1,0},{2,1},{3,2},{4,3},{5,4},{6,5},{7,6},{0,7},{9,8},{10,9},{11,1... | collective-permute-start | bytes 313352 | tf_op jit(solution)/shard_map/ppermute | solution.py:17
  112.2 5.7 %copy-start.3 = (f32[32,32,3,255]{3,2,1,0:T(4,128)S(1)}, f32[32,32,3,255]{3,2,1,0:T(4,128)}, u32[]{:S(2)}) copy-start(f32[32,32,3,255]{3,2,1,0:T(4,128)} %get-tuple-element.389) | copy-start | bytes 9400324
  112.2 5.7 %collective-permute-start.7 = (f32[34,1,3,256]{3,2,1,0:T(4,128)S(1)}, f32[34,1,3,256]{3,2,1,0:T(4,128)S(1)}, u32[]{:S(2)}, u32[]{:S(2)}) collective-permute-start(f32[34,1,3,256]{3,2,1,0:T(4,128)S(1)} %get-tuple-element.379), channel_id=1, source_target_pairs={{0,1},{1,2},{2,3},{3,4},{4,5},{5,6},{6,7},{7,0},{8,9},{9,10},{10,1... | collective-permute-start | bytes 313352 | tf_op jit(solution)/shard_map/ppermute | solution.py:16
  134.5 7.1 %collective-permute-start.8 = (f32[1,32,3,256]{3,2,1,0:T(4,128)S(1)}, f32[1,32,3,256]{3,2,1,0:T(4,128)S(1)}, u32[]{:S(2)}, u32[]{:S(2)}) collective-permute-start(f32[1,32,3,256]{3,2,1,0:T(4,128)S(1)} %get-tuple-element.381), channel_id=1, source_target_pairs={{8,0},{16,8},{24,16},{0,24},{9,1},{17,9},{25,17},{1,25},{10,2},{18... | collective-permute-start | bytes 294920 | tf_op jit(solution)/shard_map/ppermute | solution.py:17
  136.8 6.8 %collective-permute-start.9 = (f32[1,32,3,256]{3,2,1,0:T(4,128)S(1)}, f32[1,32,3,256]{3,2,1,0:T(4,128)S(1)}, u32[]{:S(2)}, u32[]{:S(2)}) collective-permute-start(f32[1,32,3,256]{3,2,1,0:T(4,128)S(1)} %get-tuple-element.380), channel_id=1, source_target_pairs={{0,8},{8,16},{16,24},{24,0},{1,9},{9,17},{17,25},{25,1},{2,10},{10... | collective-permute-start | bytes 294920 | tf_op jit(solution)/shard_map/ppermute | solution.py:16
  143.6 4.1 %collective-permute-start.10 = (f32[34,1,3,256]{3,2,1,0:T(4,128)S(1)}, f32[34,1,3,256]{3,2,1,0:T(4,128)S(1)}, u32[]{:S(2)}, u32[]{:S(2)}) collective-permute-start(f32[34,1,3,256]{3,2,1,0:T(4,128)S(1)} %get-tuple-element.376), channel_id=1, source_target_pairs={{1,0},{2,1},{3,2},{4,3},{5,4},{6,5},{7,6},{0,7},{9,8},{10,9},{11,1... | collective-permute-start | bytes 313352 | tf_op jit(solution)/shard_map/ppermute | solution.py:17
  144.8 5.4 %copy-start.2 = (f32[32,32,3,255]{3,2,1,0:T(4,128)S(1)}, f32[32,32,3,255]{3,2,1,0:T(4,128)}, u32[]{:S(2)}) copy-start(f32[32,32,3,255]{3,2,1,0:T(4,128)} %get-tuple-element.383) | copy-start | bytes 9400324
  144.8 5.4 %collective-permute-start.11 = (f32[34,1,3,256]{3,2,1,0:T(4,128)S(1)}, f32[34,1,3,256]{3,2,1,0:T(4,128)S(1)}, u32[]{:S(2)}, u32[]{:S(2)}) collective-permute-start(f32[34,1,3,256]{3,2,1,0:T(4,128)S(1)} %get-tuple-element.377), channel_id=1, source_target_pairs={{0,1},{1,2},{2,3},{3,4},{4,5},{5,6},{6,7},{7,0},{8,9},{9,10},{10,1... | collective-permute-start | bytes 313352 | tf_op jit(solution)/shard_map/ppermute | solution.py:16
  167.8 6.9 %collective-permute-start.12 = (bf16[2,32,3,256]{3,2,1,0:T(4,128)(2,1)S(1)}, bf16[2,32,3,256]{3,2,1,0:T(4,128)(2,1)S(1)}, u32[]{:S(2)}, u32[]{:S(2)}) collective-permute-start(bf16[2,32,3,256]{3,2,1,0:T(4,128)(2,1)S(1)} %get-tuple-element.396), channel_id=1, source_target_pairs={{0,8},{8,16},{16,24},{24,0},{1,9},{9,17},{17,25},{25,1},{2,10},{10... | collective-permute-start | bytes 294920 | tf_op jit(solution)/shard_map/ppermute | solution.py:16
  169.1 6.4 %collective-permute-start.13 = (bf16[2,32,3,256]{3,2,1,0:T(4,128)(2,1)S(1)}, bf16[2,32,3,256]{3,2,1,0:T(4,128)(2,1)S(1)}, u32[]{:S(2)}, u32[]{:S(2)}) collective-permute-start(bf16[2,32,3,256]{3,2,1,0:T(4,128)(2,1)S(1)} %get-tuple-element.397), channel_id=1, source_target_pairs={{8,0},{16,8},{24,16},{0,24},{9,1},{17,9},{25,17},{1,25},{10,2},{18... | collective-permute-start | bytes 294920 | tf_op jit(solution)/shard_map/ppermute | solution.py:17
  175.7 5.7 %collective-permute-start.14 = (bf16[36,2,3,256]{3,2,1,0:T(4,128)(2,1)S(1)}, bf16[36,2,3,256]{3,2,1,0:T(4,128)(2,1)S(1)}, u32[]{:S(2)}, u32[]{:S(2)}) collective-permute-start(bf16[36,2,3,256]{3,2,1,0:T(4,128)(2,1)S(1)} %get-tuple-element.394), channel_id=1, source_target_pairs={{0,1},{1,2},{2,3},{3,4},{4,5},{5,6},{6,7},{7,0},{8,9},{9,10},{10,1... | collective-permute-start | bytes 331784 | tf_op jit(solution)/shard_map/ppermute | solution.py:16
  175.7 5.7 %collective-permute-start.15 = (bf16[36,2,3,256]{3,2,1,0:T(4,128)(2,1)S(1)}, bf16[36,2,3,256]{3,2,1,0:T(4,128)(2,1)S(1)}, u32[]{:S(2)}, u32[]{:S(2)}) collective-permute-start(bf16[36,2,3,256]{3,2,1,0:T(4,128)(2,1)S(1)} %get-tuple-element.395), channel_id=1, source_target_pairs={{1,0},{2,1},{3,2},{4,3},{5,4},{6,5},{7,6},{0,7},{9,8},{10,9},{11,1... | collective-permute-start | bytes 331784 | tf_op jit(solution)/shard_map/ppermute | solution.py:17
  206.0 12.4 %all-to-all-start.1 = ((f32[32,1,144]{2,1,0:T(1,128)}), f32[32,1,144]{2,1,0:T(1,128)S(1)}, u32[]{:S(2)}, u32[]{:S(2)}) async-start(f32[32,1,144]{2,1,0:T(1,128)} %reshape.1715), calls=%async_computation.1 | async-start | bytes 65536 | tf_op jit(solution)/shard_map/all_to_all | solution.py:126
where the time goes:
time: 221 us; the launch traced here: 220 us
  other arithmetic  63.8 us (29%)
  local copies, waits for them, and re-layouts  50.7 us (23%)
  waiting for transfers between devices  38.9 us (18%)
  starting transfers between devices  34.1 us (15%)
  matrix products  31 us (14%)
    ppermute x8, waiting for transfers between devices, padded_2(): before = lax.ppermute(last, axis, up)  22.1 us
    dot_general x4, matrix products, spread_block(): jnp.einsum('pa,pb->ab', plane_wts, push_rows.astype(jnp.bfloat16), prefer...  19.1 us
    ppermute x8, starting transfers between devices, padded_2(): after = lax.ppermute(first, axis, down)  19 us
    convert_element_type x1, other arithmetic, body(): rounded = padded_2(field.astype(jnp.bfloat16), (('gx', 0), ('gy', 1)), 2)  17.5 us
    add x1, other arithmetic, laplace_of(): return center + viscosity * (result - 6.0 * center)  16.6 us
    unnamed x18, local copies, waits for them, and re-layouts  14.7 us
    slice x4, local copies, waits for them, and re-layouts, laplace_of(): result = result + jnp.roll(center, -1, 3) + jnp.roll(center, 1, 3)  12.9 us
    dot_general x4, matrix products, gather_block(): jnp.dot(plane_wts, flat_vel, preferred_element_type=jnp.float32)  11.9 us
  transfers between devices with their start and end apart: 18, of which 13 were waited for; matrix products, arithmetic and copies ran while one was open for 13% of the time, Pallas kernels for 0%

commit v1 on v0

v1 whole, which is shorter than its diff:
```python
import functools

import jax
import jax.numpy as jnp
from jax import lax
from jax.experimental import pallas as pl
from jax.experimental.pallas import tpu as pltpu
from jax.sharding import PartitionSpec as P

viscosity = 0.15
F32 = jnp.float32
BF16 = jnp.bfloat16
LANES = 128
REACH = 4

SIDES = ((-1, -1), (-1, 0), (-1, 1), (1, -1), (1, 0), (1, 1), (0, -1), (0, 1))


def iota(shape, dim):
    return lax.broadcasted_iota(jnp.int32, shape, dim)


def piece_at(tile_of, start, width, target):
    first, off = divmod(start, LANES)
    shift = (target - off) % LANES
    out = pltpu.roll(tile_of(first), shift, 1) if shift else tile_of(first)
    spill = off + width - LANES
    if spill > 0:
        rest = tile_of(first + 1)
        rest = pltpu.roll(rest, shift, 1) if shift else rest
        lane = iota(out.shape, 1)
        begin = (target + width - spill) % LANES
        end = begin + spill
        inside = (lane >= begin) & (lane < end)
        if end > LANES:
            inside = inside | (lane < end - LANES)
        out = jnp.where(inside, rest, out)
    return out


def lane_mask(shape, begin, end):
    lane = iota(shape, 1)
    return (lane >= begin) & (lane < end)


def front_kernel(dims, counts, loads, fractions, corners, neighbours, out, rows, buckets):
    groups_x, groups_y, cells_x, cells_y, cells_z, per_peer = dims
    devices = groups_x * groups_y
    slots = loads.shape[1]
    tiles = slots // LANES
    whole_x, whole_y = groups_x * cells_x, groups_y * cells_y
    position = corners[...].astype(F32) + fractions[...]
    for c in range(3):
        rows[2 * c : 2 * c + 1, :] = loads[c : c + 1, :]
        rows[2 * c + 1 : 2 * c + 2, :] = position[c : c + 1, :]
    rows[6:8, :] = jnp.zeros((2, slots), F32)
    sub = iota((8, LANES), 0)
    lane = iota((8, LANES), 1)
    even = (sub % 2) == 0
    stiffness = jnp.where(sub == 1, 2.0 / whole_x, jnp.where(sub == 3, 2.0 / whole_y, 2.0 / cells_z))
    stiffness = jnp.where((sub % 2 == 1) & (sub < 6), stiffness, 0.0).astype(F32)

    def force(t, _):
        at = pl.ds(pl.multiple_of(t * LANES, LANES), LANES)
        index = jnp.broadcast_to(neighbours[0:1, at], (8, LANES))
        high, low = index // LANES, index % LANES
        here = rows[:, at]
        partner = jnp.zeros((8, LANES), F32)
        for h in range(tiles):
            picked = jnp.take_along_axis(rows[:, h * LANES : (h + 1) * LANES], low, axis=1)
            partner = jnp.where(high == h, picked, partner)
        pull = pltpu.roll(stiffness * (partner - here), 7, 0)
        rows[:, at] = jnp.where(even, here + pull, here)
        return 0

    lax.fori_loop(0, tiles, force, 0)

    period = jnp.where(sub == 1, float(whole_x), jnp.where(sub == 3, float(whole_y), 4.0e9)).astype(F32)
    for d in range(devices):
        a, b = divmod(d, groups_y)
        got = piece_at(lambda i: rows[:, i * LANES : (i + 1) * LANES], d * per_peer, per_peer, 0)
        base = jnp.where(sub == 1, float(a * cells_x), jnp.where(sub == 3, float(b * cells_y), 0.0)).astype(F32)
        moved = got - base
        moved = jnp.where(moved > 0.5 * period, moved - period, moved)
        moved = jnp.where(moved < -0.5 * period, moved + period, moved)
        live = lane < counts[d]
        buckets[d] = jnp.where(even, jnp.where(live, got, 0.0), moved)

    tiles_out = out.shape[2] // LANES

    def send(d, _):
        a, b = d // groups_y, d % groups_y
        acc = [jnp.zeros((8, LANES), F32) for _ in range(tiles_out)]

        def put(value, start, rows_ok):
            m, off = divmod(start, LANES)
            value = pltpu.roll(value, off, 1) if off else value
            ok = lane_mask((8, LANES), off, min(off + per_peer, LANES))
            ok = ok if rows_ok is None else ok & rows_ok
            acc[m] = jnp.where(ok, value, acc[m])
            if off + per_peer > LANES:
                ok = lane_mask((8, LANES), 0, off + per_peer - LANES)
                ok = ok if rows_ok is None else ok & rows_ok
                acc[m + 1] = jnp.where(ok, value, acc[m + 1])

        for k, (dx, dy) in enumerate(SIDES):
            owner = ((a + dx + groups_x) % groups_x) * groups_y + (b + dy + groups_y) % groups_y
            put(buckets[owner], k * per_peer, None)
        own = buckets[d]
        for c in range(3):
            put(pltpu.roll(own, 6 - 2 * c, 0), c * per_peer, sub >= 6)
        for m in range(tiles_out):
            out[d, :, m * LANES : (m + 1) * LANES] = acc[m]
        return 0

    lax.fori_loop(0, devices, send, 0)


def quarter_sine(t):
    half_pi = 1.5707963267948966
    coeffs = []
    term = half_pi
    for n in range(8):
        coeffs.append(term)
        term = -term * half_pi * half_pi / ((2 * n + 2) * (2 * n + 3))
    square = t * t
    total = jnp.full_like(t, coeffs[-1])
    for coeff in coeffs[-2::-1]:
        total = total * square + coeff
    return total * t


def main_kernel(
    dims, got, velocity, x_low, x_high, y_low, y_high, field, back,
    lists, floors, sines, cosines, wts, push, depth, side_wts, grid, mid, rounded, own_vel, values, sem_in, sem_out,
):
    groups_x, groups_y, cells_x, cells_y, cells_z, per_peer = dims
    sources = groups_x * groups_y
    points = sources * per_peer
    block = wts.shape[1]
    blocks = points // block
    ext_x, ext_y = cells_x + 2 * REACH, cells_y + 2 * REACH
    inner_x = cells_x + REACH
    load_vel = pltpu.make_async_copy(velocity, own_vel, sem_in)
    load_vel.start()
    sub = iota((8, LANES), 0)

    for k in range(len(SIDES) + 1):
        for m in range(points // LANES):
            acc = jnp.zeros((8, LANES), F32)
            for s in range(m * LANES // per_peer, -(-(m + 1) * LANES // per_peer)):
                at = s * per_peer - m * LANES
                ok = lane_mask((8, LANES), max(at, 0), min(at + per_peer, LANES))
                tile_of = lambda i, s=s: got[s, :, i * LANES : (i + 1) * LANES]
                if k < len(SIDES):
                    acc = jnp.where(ok, piece_at(tile_of, k * per_peer, per_peer, at % LANES), acc)
                else:
                    for c in range(3):
                        value = piece_at(tile_of, c * per_peer, per_peer, at % LANES)
                        value = pltpu.roll(value, (2 * c - 6) % 8, 0)
                        acc = jnp.where(ok & (sub // 2 == c), value, acc)
            lists[k, :, m * LANES : (m + 1) * LANES] = acc
        position = lists[k]
        floor = jnp.floor(position)
        fraction = position - floor
        floors[k] = floor
        sines[k] = quarter_sine(fraction)
        cosines[k] = quarter_sine(1.0 - fraction)

    def weights(k, c, at):
        row = slice(2 * c + 1, 2 * c + 2)
        s, co = sines[k, row, at], cosines[k, row, at]
        return (0.25 * (1.0 - s), 0.25 * (1.0 + co), 0.25 * (1.0 + s), 0.25 * (1.0 - co))

    def table(coordinate, cells, wt):
        out = jnp.zeros(jnp.broadcast_shapes(coordinate.shape, cells[0].shape), F32)
        for cell, w in zip(cells, wt):
            out = jnp.where(coordinate == cell, w, out)
        return out

    def coord(rows, lanes, f):
        return f(iota((rows, lanes), 0)).astype(F32)

    def along_x(k, at, lanes, first, count, shift):
        cell = floors[k, 1:2, at] + float(shift)
        rows = -(-count // 8) * 8
        return table(coord(rows, lanes, lambda r: r + first), [cell + float(i) for i in range(4)], weights(k, 0, at))

    def along_y(k, at, lanes, rows, rule, shift):
        cell = floors[k, 3:4, at] + float(shift)
        return table(coord(rows, lanes, rule), [cell + float(i) for i in range(4)], weights(k, 1, at))

    def push_rows(k, at, to, lanes, keep):
        cell = floors[k, 5:6, at]
        cells = []
        for i in range(4):
            moved = cell + float(i)
            cells.append(jnp.where(moved >= float(cells_z), moved - float(cells_z), moved))
        step = 64
        wt = weights(k, 2, at)
        for z in range(0, cells_z, step):
            part = table(coord(step, lanes, lambda r: r + z), cells, wt)
            if keep:
                depth[z : z + step, to] = part
            for c in range(3):
                force = lists[k, 2 * c : 2 * c + 1, at]
                push[c, z : z + step, to] = (part * force).astype(BF16)

    chunk = 256

    def circle(r):
        return jnp.where(r < cells_y + REACH, r, r - ext_y)

    def build_own(base):
        def step(i, _):
            at = pl.ds(pl.multiple_of(base + i * chunk, chunk), chunk)
            to = pl.ds(pl.multiple_of(i * chunk, chunk), chunk)
            k = len(SIDES)
            ax = along_x(k, at, chunk, -2, inner_x, 0)
            ay = along_y(k, at, chunk, ext_y, circle, 0)
            for x in range(0, inner_x, 2):
                pair = jnp.concatenate([ax[x : x + 1] * ay, ax[x + 1 : x + 2] * ay], axis=0)
                wts[x * ext_y : (x + 2) * ext_y, to] = pair.astype(BF16)
            push_rows(k, at, to, chunk, True)
            return 0

        lax.fori_loop(0, block // chunk, step, 0)

    def dot_t(a, b):
        return lax.dot_general(a, b, (((1,), (1,)), ((), ())), preferred_element_type=F32)

    for base in range(0, points, block):
        build_own(base)

        def spread_own(c, _, base=base):
            total = dot_t(wts[...], push[c]).reshape(inner_x, ext_y, cells_z)
            if base == 0:
                grid[2 : 2 + inner_x, c] = total
                grid[0:2, c] = jnp.zeros((2, ext_y, cells_z), F32)
                grid[2 + inner_x :, c] = jnp.zeros((2, ext_y, cells_z), F32)
            else:
                grid[2 : 2 + inner_x, c] += total
            return 0

        lax.fori_loop(0, 3, spread_own, 0)

    edge = REACH + 2
    for k, (dx, dy) in enumerate(SIDES):
        for base in range(0, points, block):
            first = -REACH if dx < 0 else cells_x - 2
            tile_a = 0 if dy < 0 else cells_y - 8

            def step(i, _, k=k, dx=dx, dy=dy, base=base, first=first, tile_a=tile_a):
                at = pl.ds(pl.multiple_of(base + i * chunk, chunk), chunk)
                to = pl.ds(pl.multiple_of(i * chunk, chunk), chunk)
                if dx:
                    ax = along_x(k, at, chunk, first, edge, dx * cells_x)
                    ay = along_y(k, at, chunk, ext_y, circle, dy * cells_y)
                    for x in range(0, edge, 2):
                        pair = jnp.concatenate([ax[x : x + 1] * ay, ax[x + 1 : x + 2] * ay], axis=0)
                        side_wts[x * ext_y : (x + 2) * ext_y, to] = pair.astype(BF16)
                else:
                    ax = along_x(k, at, chunk, -2, inner_x, 0)
                    rule = lambda r: circle(jnp.where(r < 8, r + tile_a, r - 8 + cells_y))
                    ay = along_y(k, at, chunk, 16, rule, dy * cells_y)
                    for x in range(inner_x):
                        side_wts[x * 16 : (x + 1) * 16, to] = (ax[x : x + 1] * ay).astype(BF16)
                push_rows(k, at, to, chunk, False)
                return 0

            lax.fori_loop(0, block // chunk, step, 0)

            def spread(c, _, dx=dx, first=first, tile_a=tile_a):
                if dx:
                    total = dot_t(side_wts[0 : edge * ext_y, :], push[c]).reshape(edge, ext_y, cells_z)
                    grid[first + REACH : first + REACH + edge, c] += total
                else:
                    total = dot_t(side_wts[...], push[c]).reshape(inner_x, 2, 8, cells_z)
                    grid[2 : 2 + inner_x, c, tile_a : tile_a + 8] += total[:, 0]
                    grid[2 : 2 + inner_x, c, cells_y : cells_y + 8] += total[:, 1]
                return 0

            lax.fori_loop(0, 3, spread, 0)

    load_vel.wait()

    def add_velocity(x, _):
        for c in range(3):
            grid[x + REACH, c, 0:cells_y] += own_vel[x, c]
        return 0

    lax.fori_loop(0, cells_x, add_velocity, 0)

    def add_edges(x, _):
        for c in range(3):
            grid[x, c, 0:cells_y] += x_low[x, c].astype(F32)
            grid[x + REACH + cells_x, c, 0:cells_y] += x_high[x, c].astype(F32)
        return 0

    lax.fori_loop(0, REACH, add_edges, 0)

    def add_sides(x, _):
        for c in range(3):
            pair = jnp.concatenate([y_high[x, c].astype(F32), y_low[x, c].astype(F32)], axis=0)
            grid[x, c, cells_y:ext_y] += pair
        return 0

    lax.fori_loop(0, ext_x, add_sides, 0)

    def swept(ref, x, c):
        center = ref[x, c]
        total = ref[x - 1, c] + ref[x + 1, c]
        total = total + pltpu.roll(center, 1, 0) + pltpu.roll(center, ext_y - 1, 0)
        total = total + pltpu.roll(center, 1, 1) + pltpu.roll(center, cells_z - 1, 1)
        return center + viscosity * (total - 6.0 * center)

    def first_sweep(x, _):
        for c in range(3):
            mid[x, c] = swept(grid, x, c)
        return 0

    lax.fori_loop(1, ext_x - 1, first_sweep, 0)

    def second_sweep(i, _):
        for c in range(3):
            two = [swept(mid, 2 + 2 * i, c), swept(mid, 3 + 2 * i, c)]
            grid[2 + 2 * i, c] = two[0]
            grid[3 + 2 * i, c] = two[1]
            at = pl.ds(pl.multiple_of(i * 2 * ext_y, 2 * ext_y), 2 * ext_y)
            rounded[c, at, :] = jnp.concatenate(two, axis=0).astype(BF16)
        return 0

    lax.fori_loop(0, inner_x // 2, second_sweep, 0)
    store = pltpu.make_async_copy(grid.at[REACH : REACH + cells_x, :, 0:cells_y, :], field, sem_out)
    store.start()

    values[3:8, :] = jnp.zeros((5, points), F32)
    for base in range(0, points, block):
        if blocks > 1:
            build_own(base)
        for c in range(3):
            mixed = lax.dot_general(rounded[c], wts[...], (((0,), (0,)), ((), ())), preferred_element_type=F32)
            values[c : c + 1, base : base + block] = jnp.sum(mixed * depth[...], axis=0, keepdims=True)
    for s in range(sources):
        back[s] = piece_at(lambda i: values[:, i * LANES : (i + 1) * LANES], s * per_peer, per_peer, 0)
    store.wait()


def last_kernel(per_peer, counts, got, out):
    devices = got.shape[0]
    for m in range(out.shape[1] // LANES):
        acc = jnp.zeros((8, LANES), F32)
        for s in range(m * LANES // per_peer, -(-(m + 1) * LANES // per_peer)):
            at = s * per_peer - m * LANES
            lane = iota((8, LANES), 1)
            ok = (lane >= max(at, 0)) & (lane < jnp.minimum(at + counts[s], min(at + per_peer, LANES)))
            value = got[s]
            value = pltpu.roll(value, at % LANES, 1) if at % LANES else value
            acc = jnp.where(ok, value, acc)
        out[:, m * LANES : (m + 1) * LANES] = acc[0:3]


def body(velocity, fiber_loads, fractions, corners, neighbours, counts):
    groups_x = lax.axis_size("gx")
    groups_y = lax.axis_size("gy")
    devices = groups_x * groups_y
    slots = fiber_loads.shape[1]
    per_peer = slots // devices
    cells_x, cells_y, cells_z = (velocity.shape[0], velocity.shape[1], velocity.shape[3])
    dims = (groups_x, groups_y, cells_x, cells_y, cells_z, per_peer)
    both = ("gx", "gy")
    width = -(-len(SIDES) * per_peer // LANES) * LANES
    vmem = pl.BlockSpec(memory_space=pltpu.VMEM)
    smem = pl.BlockSpec(memory_space=pltpu.SMEM)
    hbm = pl.BlockSpec(memory_space=pl.ANY)

    payload = pl.pallas_call(
        functools.partial(front_kernel, dims),
        out_shape=jax.ShapeDtypeStruct((devices, 8, width), F32),
        in_specs=[smem] + [vmem] * 4,
        out_specs=vmem,
        scratch_shapes=[pltpu.VMEM((8, slots), F32), pltpu.VMEM((devices, 8, LANES), F32)],
        name="points_out",
    )(counts, fiber_loads, fractions, corners, neighbours.reshape(1, slots))
    received = lax.all_to_all(payload, both, split_axis=0, concat_axis=0, tiled=True)

    stored = jnp.transpose(velocity, (0, 2, 1, 3))

    def shifted(low_part, high_part, axis):
        peers = lax.axis_size(axis)
        up = [(i, (i + 1) % peers) for i in range(peers)]
        down = [(j, i) for i, j in up]
        return lax.ppermute(high_part, axis, up), lax.ppermute(low_part, axis, down)

    x_first = stored[:REACH].astype(BF16)
    x_last = stored[cells_x - REACH :].astype(BF16)
    x_low, x_high = shifted(x_first, x_last, "gx")
    y_first = jnp.concatenate([x_low[:, :, :REACH], stored[:, :, :REACH].astype(BF16), x_high[:, :, :REACH]], 0)
    y_last = jnp.concatenate(
        [x_low[:, :, cells_y - REACH :], stored[:, :, cells_y - REACH :].astype(BF16), x_high[:, :, cells_y - REACH :]], 0
    )
    y_low, y_high = shifted(y_first, y_last, "gy")

    block = min(slots, 1536)
    ext_x, ext_y, inner_x = cells_x + 2 * REACH, cells_y + 2 * REACH, cells_x + REACH
    lists = len(SIDES) + 1
    side_rows = max((REACH + 2) * ext_y, inner_x * 16)
    field, back = pl.pallas_call(
        functools.partial(main_kernel, dims),
        out_shape=(
            jax.ShapeDtypeStruct(stored.shape, F32),
            jax.ShapeDtypeStruct((devices, 8, LANES), F32),
        ),
        in_specs=[vmem, hbm] + [vmem] * 4,
        out_specs=(hbm, vmem),
        scratch_shapes=[
            pltpu.VMEM((lists, 8, slots), F32),
            pltpu.VMEM((lists, 8, slots), F32),
            pltpu.VMEM((lists, 8, slots), F32),
            pltpu.VMEM((lists, 8, slots), F32),
            pltpu.VMEM((inner_x * ext_y, block), BF16),
            pltpu.VMEM((3, cells_z, block), BF16),
            pltpu.VMEM((cells_z, block), F32),
            pltpu.VMEM((side_rows, block), BF16),
            pltpu.VMEM((ext_x, 3, ext_y, cells_z), F32),
            pltpu.VMEM((ext_x, 3, ext_y, cells_z), F32),
            pltpu.VMEM((3, inner_x * ext_y, cells_z), BF16),
            pltpu.VMEM(stored.shape, F32),
            pltpu.VMEM((8, slots), F32),
            pltpu.SemaphoreType.DMA(()),
            pltpu.SemaphoreType.DMA(()),
        ],
        compiler_params=pltpu.CompilerParams(vmem_limit_bytes=52 * 1024 * 1024),
        name="step",
    )(received, stored, x_low, x_high, y_low, y_high)
    returned = lax.all_to_all(back, both, split_axis=0, concat_axis=0, tiled=True)
    sampled = pl.pallas_call(
        functools.partial(last_kernel, per_peer),
        out_shape=jax.ShapeDtypeStruct((3, slots), F32),
        in_specs=[smem, vmem],
        out_specs=vmem,
        name="points_back",
    )(counts, returned)
    return (jnp.transpose(field, (0, 2, 1, 3)), sampled)


def solution(mesh):
    return jax.shard_map(
        body,
        mesh=mesh,
        in_specs=(
            P("gx", "gy", None, None),
            P(None, ("gx", "gy")),
            P(None, ("gx", "gy")),
            P(None, ("gx", "gy")),
            P(("gx", "gy")),
            P(("gx", "gy")),
        ),
        out_specs=(P("gx", "gy", None, None), P(None, ("gx", "gy"))),
        check_vma=False,
    )
```

time: 221 us -> 97.1 us (0.44)
  other arithmetic: 63.8 us -> 2.49 us
  local copies, waits for them, and re-layouts: 50.7 us -> 1.52 us
  Pallas kernels: 0 us -> 48 us
  matrix products: 31 us -> 0 us
  waiting for transfers between devices: 38.9 us -> 17.9 us
  starting transfers between devices: 34.1 us -> 13.7 us
  blocking collectives: 0 us -> 12.4 us
    pallas_call x0 -> x3, Pallas kernels: none -> 48 us  [the longest x1 40.5 us: body(): pl.pallas_call(functools.partial(main_kernel, dims), out_shape=(jax.Shape...]
    dot_general x8 -> x0, matrix products: 31 us -> none  [the longest x4 19.1 us: spread_block(): jnp.einsum('pa,pb->ab', plane_wts, push_rows.astype(jnp.bfloat16), prefer...]
    add x43 -> x0, other arithmetic: 22.9 us -> none  [the longest x1 16.6 us: laplace_of(): return center + viscosity * (result - 6.0 * center)]
    convert_element_type x19 -> x0, other arithmetic: 20.9 us -> none  [the longest x1 17.5 us: body(): rounded = padded_2(field.astype(jnp.bfloat16), (('gx', 0), ('gy', 1)), 2)]
    slice x45 -> x4, local copies, waits for them, and re-layouts: 19.8 us -> 0.23 us  [the longest x1 0.16 us: body(): stored[:, :, :REACH].astype(BF16)]
    ppermute x16 -> x4, starting transfers between devices: 21.6 us -> 6.41 us  [the longest x2 6.35 us: shifted(): lax.ppermute(low_part, axis, down)]
    unnamed x18 -> x0, local copies, waits for them, and re-layouts: 14.7 us -> none
    all_to_all x0 -> x1, blocking collectives: none -> 12.4 us  [body(): lax.all_to_all(back, both, split_axis=0, concat_axis=0, tiled=True)]
  transfers between devices with their start and end apart: 18 -> 5, of which waited for: 13 -> 4; matrix products, arithmetic and copies ran while one was open for 13% -> 3% of each run, Pallas kernels for 0% -> 0%
where the time goes in v1:
time: 97.1 us; the launch traced here: 96.7 us
  Pallas kernels  48 us (49%)
  waiting for transfers between devices  17.9 us (18%)
  starting transfers between devices  13.7 us (14%)
  blocking collectives  12.4 us (13%)
  other arithmetic  2.49 us (3%)
  local copies, waits for them, and re-layouts  1.52 us (2%)
    pallas_call x1, Pallas kernels, body(): pl.pallas_call(functools.partial(main_kernel, dims), out_shape=(jax.Shape...  40.5 us
    all_to_all x1, blocking collectives, body(): lax.all_to_all(back, both, split_axis=0, concat_axis=0, tiled=True)  12.4 us
    ppermute x2, waiting for transfers between devices, shifted(): lax.ppermute(high_part, axis, up)  10.4 us
    ppermute x2, waiting for transfers between devices, shifted(): lax.ppermute(low_part, axis, down)  7.51 us
    all_to_all x1, starting transfers between devices, body(): lax.all_to_all(payload, both, split_axis=0, concat_axis=0, tiled=True)  7.33 us
    ppermute x2, starting transfers between devices, shifted(): lax.ppermute(low_part, axis, down)  6.35 us
    pallas_call x1, Pallas kernels, body(): pl.pallas_call(functools.partial(front_kernel, dims), out_shape=jax.Shape...  5.88 us
    another operation x1, other arithmetic  2.13 us
  transfers between devices with their start and end apart: 5, of which 4 were waited for; matrix products, arithmetic and copies ran while one was open for 3% of the time, Pallas kernels for 0%

profile of v1, /device:TPU:0, one launch (start us, length us, event | category | flops | bytes accessed | tf_op | source)
XLA Modules:
  0.0 96.7 jit_solution(2450024915185228939)
XLA Ops:
  0.6 1.3 %reshape.7.neighbours = s32[1,1536]{1,0:T(1,128)} reshape(s32[1536]{0:T(1024)} %param.10) | data formatting | bytes 12288 | tf_op jit(solution)/shard_map/reshape | solution.py:384
  1.9 5.9 %points_out.1 = f32[32,8,384]{2,1,0:T(8,128)} custom-call(s32[32]{0:T(128)} %counts.3, f32[3,1536]{1,0:T(4,128)} %loads.1, f32[3,1536]{1,0:T(4,128)} %fractions.1, s32[3,1536]{1,0:T(4,128)} %corners.1, s32[1,1536]{1,0:T(1,128)} %reshape.7.neighbours), custom_call_target="tpu_custom_call" | custom-call | tf_op jit(solution)/shard_map/points_out/pallas_call | solution.py:377
  7.8 7.3 %all-to-all-start = ((f32[32,8,384]{2,1,0:T(8,128)}), f32[32,8,384]{2,1,0:T(8,128)S(1)}, u32[]{:S(2)}, u32[]{:S(2)}) async-start(f32[32,8,384]{2,1,0:T(8,128)} %points_out.1), calls=%async_computation | async-start | bytes 786432 | tf_op jit(solution)/shard_map/all_to_all | solution.py:385
  15.1 2.1 %bitcast_convert_fusion = bf16[32,3,32,256]{3,2,1,0:T(8,128)(2,1)S(1)} fusion(f32[32,32,3,256]{3,1,2,0:T(8,128)} %param.6), kind=kLoop, calls=%fused_computation.2 | loop fusion | flops 786432 | bytes 4718592 | tf_op jit(solution)/shard_map/convert.3
  17.3 3.7 %collective-permute-start.1 = (bf16[4,3,32,256]{3,2,1,0:T(8,128)(2,1)S(1)}, bf16[4,3,32,256]{3,2,1,0:T(8,128)(2,1)S(1)}, u32[]{:S(2)}, u32[]{:S(2)}) collective-permute-start(bf16[4,3,32,256]{3,2,1,0:T(8,128)(2,1)S(1)} %get-tuple-element.8), channel_id=1, source_target_pairs={{8,0},{16,8},{24,16},{0,24},{9,1},{17,9},{25,17},{1,25},{10,2},{18... | collective-permute-start | bytes 589832 | tf_op jit(solution)/shard_map/ppermute | solution.py:393
  21.0 0.0 collective-permute-start
  21.0 0.2 fusion
  21.1 7.4 %collective-permute-done.1.x_high = bf16[4,3,32,256]{3,2,1,0:T(8,128)(2,1)S(1)} collective-permute-done((bf16[4,3,32,256]{3,2,1,0:T(8,128)(2,1)S(1)}, bf16[4,3,32,256]{3,2,1,0:T(8,128)(2,1)S(1)}, u32[]{:S(2)}, u32[]{:S(2)}) %collective-permute-start.1) | collective-permute-done | bytes 196640 | tf_op jit(solution)/shard_map/ppermute | solution.py:393
  28.5 6.1 %collective-permute-done.x_low = bf16[4,3,32,256]{3,2,1,0:T(8,128)(2,1)S(1)} collective-permute-done((bf16[4,3,32,256]{3,2,1,0:T(8,128)(2,1)S(1)}, bf16[4,3,32,256]{3,2,1,0:T(8,128)(2,1)S(1)}, u32[]{:S(2)}, u32[]{:S(2)}) %collective-permute-start) | collective-permute-done | bytes 196640 | tf_op jit(solution)/shard_map/ppermute | solution.py:393
  34.7 0.2 pad_maximum_fusion
  34.9 0.1 collective-permute-start.2
  34.9 0.2 pad_maximum_fusion.1
  35.1 2.7 %collective-permute-start.3 = (bf16[40,3,4,256]{3,2,1,0:T(4,128)(2,1)S(1)}, bf16[40,3,4,256]{3,2,1,0:T(4,128)(2,1)S(1)}, u32[]{:S(2)}, u32[]{:S(2)}) collective-permute-start(bf16[40,3,4,256]{3,2,1,0:T(4,128)(2,1)S(1)} %pad_maximum_fusion.1), channel_id=1, source_target_pairs={{1,0},{2,1},{3,2},{4,3},{5,4},{6,5},{7,6},{0,7},{9,8},{10,9},{11,1... | collective-permute-start | bytes 737288 | tf_op jit(solution)/shard_map/ppermute | solution.py:393
  37.8 4.2 %collective-permute-done.2.y_low = bf16[40,3,4,256]{3,2,1,0:T(4,128)(2,1)S(1)} collective-permute-done((bf16[40,3,4,256]{3,2,1,0:T(4,128)(2,1)S(1)}, bf16[40,3,4,256]{3,2,1,0:T(4,128)(2,1)S(1)}, u32[]{:S(2)}, u32[]{:S(2)}) %collective-permute-start.2) | collective-permute-done | bytes 245792 | tf_op jit(solution)/shard_map/ppermute | solution.py:393
  42.0 0.1 collective-permute-done.3.y_high
  42.2 0.0 all-to-all-done.got
  42.2 40.5 %step.1 = (f32[32,3,32,256]{3,2,1,0:T(8,128)}, f32[32,8,128]{2,1,0:T(8,128)S(1)}) custom-call(f32[32,8,384]{2,1,0:T(8,128)S(1)} %all-to-all-done.got, f32[32,3,32,256]{3,2,1,0:T(8,128)} %bitcast.3, bf16[4,3,32,256]{3,2,1,0:T(8,128)(2,1)S(1)} %collective-permute-done.x_low, bf16[4,3,32,256]{3,2,1,0:T(8,128)(2,1)S(1)} %collective-permute-done.1.x_high, ...), custom_call_target="tpu_custom_call" | custom-call | tf_op jit(solution)/shard_map/step/pallas_call | solution.py:408
  82.7 12.4 %all_to_all.10.got = f32[32,8,128]{2,1,0:T(8,128)} all-to-all(f32[32,8,128]{2,1,0:T(8,128)S(1)} %get-tuple-element.5), channel_id=1, replica_groups=mesh['gx'=4,'gy'=8] {'gx','gy'}, dimensions={0} | all-to-all | bytes 262144 | tf_op jit(solution)/shard_map/all_to_all | solution.py:436
  95.1 1.6 %points_back.1 = f32[3,1536]{1,0:T(4,128)} custom-call(s32[32]{0:T(128)} %counts.3, f32[32,8,128]{2,1,0:T(8,128)} %all_to_all.10.got), custom_call_target="tpu_custom_call" | custom-call | tf_op jit(solution)/shard_map/points_back/pallas_call | solution.py:437
  (3 shorter events, 0.1 us)
Async XLA Ops:
  7.8 34.4 %all-to-all-start = ((f32[32,8,384]{2,1,0:T(8,128)}), f32[32,8,384]{2,1,0:T(8,128)S(1)}, u32[]{:S(2)}, u32[]{:S(2)}) async-start(f32[32,8,384]{2,1,0:T(8,128)} %points_out.1), calls=%async_computation | async-start | bytes 786432 | tf_op jit(solution)/shard_map/all_to_all | solution.py:385
  17.3 11.2 %collective-permute-start.1 = (bf16[4,3,32,256]{3,2,1,0:T(8,128)(2,1)S(1)}, bf16[4,3,32,256]{3,2,1,0:T(8,128)(2,1)S(1)}, u32[]{:S(2)}, u32[]{:S(2)}) collective-permute-start(bf16[4,3,32,256]{3,2,1,0:T(8,128)(2,1)S(1)} %get-tuple-element.8), channel_id=1, source_target_pairs={{8,0},{16,8},{24,16},{0,24},{9,1},{17,9},{25,17},{1,25},{10,2},{18... | collective-permute-start | bytes 589832 | tf_op jit(solution)/shard_map/ppermute | solution.py:393
  21.0 13.7 %collective-permute-start = (bf16[4,3,32,256]{3,2,1,0:T(8,128)(2,1)S(1)}, bf16[4,3,32,256]{3,2,1,0:T(8,128)(2,1)S(1)}, u32[]{:S(2)}, u32[]{:S(2)}) collective-permute-start(bf16[4,3,32,256]{3,2,1,0:T(8,128)(2,1)S(1)} %get-tuple-element.9), channel_id=1, source_target_pairs={{0,8},{8,16},{16,24},{24,0},{1,9},{9,17},{17,25},{25,1},{2,10},{10... | collective-permute-start | bytes 589832 | tf_op jit(solution)/shard_map/ppermute | solution.py:393
  34.9 7.2 %collective-permute-start.2 = (bf16[40,3,4,256]{3,2,1,0:T(4,128)(2,1)S(1)}, bf16[40,3,4,256]{3,2,1,0:T(4,128)(2,1)S(1)}, u32[]{:S(2)}, u32[]{:S(2)}) collective-permute-start(bf16[40,3,4,256]{3,2,1,0:T(4,128)(2,1)S(1)} %pad_maximum_fusion), channel_id=1, source_target_pairs={{0,1},{1,2},{2,3},{3,4},{4,5},{5,6},{6,7},{7,0},{8,9},{9,10},{10,1... | collective-permute-start | bytes 737288 | tf_op jit(solution)/shard_map/ppermute | solution.py:393
  35.1 7.1 %collective-permute-start.3 = (bf16[40,3,4,256]{3,2,1,0:T(4,128)(2,1)S(1)}, bf16[40,3,4,256]{3,2,1,0:T(4,128)(2,1)S(1)}, u32[]{:S(2)}, u32[]{:S(2)}) collective-permute-start(bf16[40,3,4,256]{3,2,1,0:T(4,128)(2,1)S(1)} %pad_maximum_fusion.1), channel_id=1, source_target_pairs={{1,0},{2,1},{3,2},{4,3},{5,4},{6,5},{7,6},{0,7},{9,8},{10,9},{11,1... | collective-permute-start | bytes 737288 | tf_op jit(solution)/shard_map/ppermute | solution.py:393

commit v2 on v1

v2 whole, which is shorter than its diff:
```python
import functools

import jax
import jax.numpy as jnp
from jax import lax
from jax.experimental import pallas as pl
from jax.experimental.pallas import tpu as pltpu
from jax.sharding import PartitionSpec as P


viscosity = 0.15
F32 = jnp.float32
BF16 = jnp.bfloat16
LANES = 128
MIB = 1024 * 1024
STEP_MIB = 58
REACH = 4

SIDES = ((-1, -1), (-1, 0), (-1, 1), (1, -1), (1, 0), (1, 1), (0, -1), (0, 1))


def iota(shape, dim):
    return lax.broadcasted_iota(jnp.int32, shape, dim)


def piece_at(tile_of, start, width, target):
    first, off = divmod(start, LANES)
    shift = (target - off) % LANES
    out = pltpu.roll(tile_of(first), shift, 1) if shift else tile_of(first)
    spill = off + width - LANES
    if spill > 0:
        rest = tile_of(first + 1)
        rest = pltpu.roll(rest, shift, 1) if shift else rest
        lane = iota(out.shape, 1)
        begin = (target + width - spill) % LANES
        end = begin + spill
        inside = (lane >= begin) & (lane < end)
        if end > LANES:
            inside = inside | (lane < end - LANES)
        out = jnp.where(inside, rest, out)
    return out


def lane_mask(shape, begin, end):
    lane = iota(shape, 1)
    return (lane >= begin) & (lane < end)


def front_kernel(dims, counts, loads, fractions, corners, neighbours, out, rows, buckets, reach, order):
    groups_x, groups_y, cells_x, cells_y, cells_z, per_peer = dims
    devices = groups_x * groups_y
    slots = loads.shape[1]
    tiles = slots // LANES
    whole_x, whole_y = groups_x * cells_x, groups_y * cells_y
    position = corners[...].astype(F32) + fractions[...]
    for c in range(3):
        rows[2 * c : 2 * c + 1, :] = loads[c : c + 1, :]
        rows[2 * c + 1 : 2 * c + 2, :] = position[c : c + 1, :]
    rows[6:8, :] = jnp.zeros((2, slots), F32)
    sub = iota((8, LANES), 0)
    lane = iota((8, LANES), 1)
    even = (sub % 2) == 0
    stiffness = jnp.where(sub == 1, 2.0 / whole_x, jnp.where(sub == 3, 2.0 / whole_y, 2.0 / cells_z))
    stiffness = jnp.where((sub % 2 == 1) & (sub < 6), stiffness, 0.0).astype(F32)

    def force(t, _):
        at = pl.ds(pl.multiple_of(t * LANES, LANES), LANES)
        index = jnp.broadcast_to(neighbours[at].reshape(1, LANES), (8, LANES))
        high, low = index // LANES, index % LANES
        here = rows[:, at]
        partner = jnp.zeros((8, LANES), F32)
        for h in range(tiles):
            picked = jnp.take_along_axis(rows[:, h * LANES : (h + 1) * LANES], low, axis=1)
            partner = jnp.where(high == h, picked, partner)
        pull = pltpu.roll(stiffness * (partner - here), 7, 0)
        rows[:, at] = jnp.where(even, here + pull, here)
        return 0

    lax.fori_loop(0, tiles, force, 0, unroll=4)

    far = 1.0e9
    low_x = sum([jnp.where(sub == k, cells_x - REACH - 3.0 if dx < 0 else -far, 0.0) for k, (dx, _) in enumerate(SIDES)])
    end_x = sum([jnp.where(sub == k, float(REACH) if dx > 0 else far, 0.0) for k, (dx, _) in enumerate(SIDES)])
    low_y = sum([jnp.where(sub == k, cells_y - REACH - 3.0 if dy < 0 else -far, 0.0) for k, (_, dy) in enumerate(SIDES)])
    end_y = sum([jnp.where(sub == k, float(REACH) if dy > 0 else far, 0.0) for k, (_, dy) in enumerate(SIDES)])
    period = jnp.where(sub == 1, float(whole_x), jnp.where(sub == 3, float(whole_y), 4.0e9)).astype(F32)
    for d in range(devices):
        a, b = divmod(d, groups_y)
        got = piece_at(lambda i: rows[:, i * LANES : (i + 1) * LANES], d * per_peer, per_peer, 0)
        base = jnp.where(sub == 1, float(a * cells_x), jnp.where(sub == 3, float(b * cells_y), 0.0)).astype(F32)
        moved = got - base
        moved = jnp.where(moved > 0.5 * period, moved - period, moved)
        moved = jnp.where(moved < -0.5 * period, moved + period, moved)
        live = lane < counts[d]
        local = jnp.where(live, jnp.where(even, got, moved), jnp.where(even | (lane >= per_peer), 0.0, moved))
        buckets[d] = local
        at_x = jnp.broadcast_to(local[1:2], (8, LANES))
        at_y = jnp.broadcast_to(local[3:4], (8, LANES))
        near = live & (at_x >= low_x) & (at_x < end_x) & (at_y >= low_y) & (at_y < end_y)
        reach[8 * d : 8 * d + 8, :] = jnp.where(near, 1.0, 0.0)

    before = jnp.where(iota((LANES, LANES), 0) <= iota((LANES, LANES), 1), 1.0, 0.0).astype(BF16)
    reach[...] = jnp.dot(reach[...].astype(BF16), before, preferred_element_type=F32)
    starts = sum([jnp.where(sub == k, (k * per_peer) % LANES, 0) for k in range(len(SIDES))])
    rank = ((lane - starts + LANES) % LANES).astype(F32)

    def find(d, _):
        upto = reach[pl.ds(pl.multiple_of(8 * d, 8), 8), :]
        spot = jnp.zeros((8, LANES), jnp.int32)
        for bit in (32, 16, 8, 4, 2, 1):
            seen = jnp.take_along_axis(upto, spot + (bit - 1), axis=1)
            spot = jnp.where(seen <= rank, spot + bit, spot)
        order[d] = spot
        return 0

    lax.fori_loop(0, devices, find, 0, unroll=16)
    tiles_out = out.shape[2] // LANES

    def send(d):
        a, b = divmod(d, groups_y)
        acc = [jnp.zeros((8, LANES), F32) for _ in range(tiles_out)]

        def put(value, start, rows_ok):
            m, off = divmod(start, LANES)
            ok = lane_mask((8, LANES), off, min(off + per_peer, LANES))
            ok = ok if rows_ok is None else ok & rows_ok
            acc[m] = jnp.where(ok, value, acc[m])
            if off + per_peer > LANES:
                ok = lane_mask((8, LANES), 0, off + per_peer - LANES)
                ok = ok if rows_ok is None else ok & rows_ok
                acc[m + 1] = jnp.where(ok, value, acc[m + 1])

        counted = []
        for k, (dx, dy) in enumerate(SIDES):
            owner = ((a + dx + groups_x) % groups_x) * groups_y + (b + dy + groups_y) % groups_y
            index = jnp.broadcast_to(order[owner, k : k + 1, :], (8, LANES))
            put(jnp.take_along_axis(buckets[owner], index, axis=1), k * per_peer, None)
            counted.append(jnp.broadcast_to(reach[8 * owner + k : 8 * owner + k + 1, :], (8, LANES)))
        own = buckets[d]
        for c in range(3):
            value = pltpu.roll(own, 6 - 2 * c, 0)
            value = pltpu.roll(value, (c * per_peer) % LANES, 1) if c else value
            put(value, c * per_peer, sub >= 6)
        for k, count in enumerate(counted):
            acc[-1] = jnp.where((sub == 7) & (lane == LANES - 8 + k), count, acc[-1])
        for m in range(tiles_out):
            out[d, :, m * LANES : (m + 1) * LANES] = acc[m]

    for d in range(devices):
        send(d)


def quarter_sine(t):
    half_pi = 1.5707963267948966
    coeffs = []
    term = half_pi
    for n in range(8):
        coeffs.append(term)
        term = -term * half_pi * half_pi / ((2 * n + 2) * (2 * n + 3))
    square = t * t
    total = jnp.full_like(t, coeffs[-1])
    for coeff in coeffs[-2::-1]:
        total = total * square + coeff
    return total * t


def main_kernel(
    dims, got, velocity, x_low_in, x_high_in, y_low_in, y_high_in, field, back,
    own, floors, sines, cosines, wts, push, depth, side_wts, side_push, grid, mid, rounded, own_vel, values, x_sides, y_sides, sems,
):
    groups_x, groups_y, cells_x, cells_y, cells_z, per_peer = dims
    sources = groups_x * groups_y
    points = sources * per_peer
    block = wts.shape[1]
    blocks = points // block
    ext_x, ext_y = cells_x + 2 * REACH, cells_y + 2 * REACH
    inner_x = cells_x + REACH
    load_vel = pltpu.make_async_copy(velocity, own_vel, sems.at[0])
    load_vel.start()
    load_sides = []
    for i, ref in enumerate((x_low_in, x_high_in, y_low_in, y_high_in)):
        to = (x_sides if i < 2 else y_sides).at[i % 2]
        load_sides.append(pltpu.make_async_copy(ref, to, sems.at[2 + i]))
        load_sides[-1].start()
    sub = iota((8, LANES), 0)
    lane = iota((8, LANES), 1)

    for m in range(points // LANES):
        acc = jnp.zeros((8, LANES), F32)
        for s in range(m * LANES // per_peer, -(-(m + 1) * LANES // per_peer)):
            at = s * per_peer - m * LANES
            ok = lane_mask((8, LANES), max(at, 0), min(at + per_peer, LANES))
            for c in range(3):
                value = piece_at(lambda i, s=s: got[s, :, i * LANES : (i + 1) * LANES], c * per_peer, per_peer, at % LANES)
                value = pltpu.roll(value, (2 * c - 6) % 8, 0)
                acc = jnp.where(ok & (sub // 2 == c), value, acc)
        own[:, m * LANES : (m + 1) * LANES] = acc

    def split(position):
        floor = jnp.floor(position)
        fraction = position - floor
        return floor, quarter_sine(fraction), quarter_sine(1.0 - fraction)

    floors[...], sines[...], cosines[...] = split(own[...])

    def weights(s, co):
        return (0.25 * (1.0 - s), 0.25 * (1.0 + co), 0.25 * (1.0 + s), 0.25 * (1.0 - co))

    def table(coordinate, cells, wt):
        out = jnp.zeros(jnp.broadcast_shapes(coordinate.shape, cells[0].shape), F32)
        for cell, w in zip(cells, wt):
            out = jnp.where(coordinate == cell, w, out)
        return out

    def coord(rows, lanes, f):
        return f(iota((rows, lanes), 0)).astype(F32)

    def along(cell, wt, rows, rule):
        return table(coord(rows, cell.shape[1], rule), [cell + float(i) for i in range(4)], wt)

    def push_rows(cell, wt, forces, to_push, to, keep):
        lanes = cell.shape[1]
        cells = []
        for i in range(4):
            moved = cell + float(i)
            cells.append(jnp.where(moved >= float(cells_z), moved - float(cells_z), moved))
        step = 64
        for z in range(0, cells_z, step):
            part = table(coord(step, lanes, lambda r: r + z), cells, wt)
            if keep:
                depth[z : z + step, to] = part
            for c in range(3):
                to_push[c, z : z + step, to] = (part * forces[c]).astype(BF16)

    def circle(r):
        return jnp.where(r < cells_y + REACH, r, r - ext_y)

    def pair_rows(ax, ay, x):
        return jnp.concatenate([ax[x : x + 1] * ay, ax[x + 1 : x + 2] * ay], axis=0).astype(BF16)

    chunk = 256

    def build_own(base):
        def step(i, _):
            at = pl.ds(pl.multiple_of(base + i * chunk, chunk), chunk)
            to = pl.ds(pl.multiple_of(i * chunk, chunk), chunk)
            cell = [floors[2 * c + 1 : 2 * c + 2, at] for c in range(3)]
            wt = [weights(sines[2 * c + 1 : 2 * c + 2, at], cosines[2 * c + 1 : 2 * c + 2, at]) for c in range(3)]
            ax = along(cell[0], wt[0], -(-inner_x // 8) * 8, lambda r: r - 2)
            ay = along(cell[1], wt[1], ext_y, circle)
            for x in range(0, inner_x, 2):
                wts[x * ext_y : (x + 2) * ext_y, to] = pair_rows(ax, ay, x)
            push_rows(cell[2], wt[2], [own[2 * c : 2 * c + 1, at] for c in range(3)], push, to, True)
            return 0

        lax.fori_loop(0, block // chunk, step, 0)

    def dot_t(a, b):
        return lax.dot_general(a, b, (((1,), (1,)), ((), ())), preferred_element_type=F32)

    for base in range(0, points, block):
        build_own(base)
        if base == 0:
            load_vel.wait()

        def spread_own(c, _, base=base):
            total = dot_t(wts[...], push[c]).reshape(inner_x, ext_y, cells_z)
            if base == 0:
                grid[2 : 2 + inner_x, c] = total
                grid[0:2, c] = jnp.zeros((2, ext_y, cells_z), F32)
                grid[2 + inner_x :, c] = jnp.zeros((2, ext_y, cells_z), F32)
                grid[REACH : REACH + cells_x, c, 0:cells_y] = total[2 : 2 + cells_x, 0:cells_y] + own_vel[:, c]
            else:
                grid[2 : 2 + inner_x, c] += total
            return 0

        lax.fori_loop(0, 3, spread_own, 0)

    edge = REACH + 2
    together = chunk // 8
    rounds = sources // together
    most = got[0, :, got.shape[2] - LANES :]
    for s in range(1, sources):
        most = jnp.maximum(most, got[s, :, got.shape[2] - LANES :])
    counts = [
        jnp.max(jnp.where((sub == 7) & (lane == LANES - 8 + k), most, 0.0)).astype(jnp.int32) for k in range(len(SIDES))
    ]

    def side(it, slot, k):
        dx, dy = SIDES[k]
        first = -REACH if dx < 0 else cells_x - 2
        tile_a = 0 if dy < 0 else cells_y - 8
        start = k * per_peer + (it // rounds if rounds > 1 else it) * 8
        source = (it % rounds if rounds > 1 else 0) * together
        at = pl.ds(pl.multiple_of(start // LANES * LANES, LANES), LANES)
        off = start % LANES
        parts = []
        for m in range(chunk // LANES):
            acc = jnp.zeros((8, LANES), F32)
            for i in range(LANES // 8):
                value = pltpu.roll(got[source + m * (LANES // 8) + i, :, at], (8 * i - off + LANES) % LANES, 1)
                acc = jnp.where(lane // 8 == i, value, acc)
            parts.append(acc)
        data = jnp.concatenate(parts, axis=1)
        floor, sine, cosine = split(data)
        cell = [floor[2 * c + 1 : 2 * c + 2] for c in range(3)]
        cell[0] = cell[0] + float(dx * cells_x)
        cell[1] = cell[1] + float(dy * cells_y)
        wt = [weights(sine[2 * c + 1 : 2 * c + 2], cosine[2 * c + 1 : 2 * c + 2]) for c in range(3)]
        if dx:
            ax = along(cell[0], wt[0], 8, lambda r: r + first)
            ay = along(cell[1], wt[1], ext_y, circle)
            for x in range(0, edge, 2):
                side_wts[slot, x * ext_y : (x + 2) * ext_y, :] = pair_rows(ax, ay, x)
        else:
            ax = along(cell[0], wt[0], -(-inner_x // 8) * 8, lambda r: r - 2)
            ay = along(cell[1], wt[1], 16, lambda r: circle(jnp.where(r < 8, r + tile_a, r - 8 + cells_y)))
            for x in range(inner_x):
                side_wts[slot, x * 16 : (x + 1) * 16, :] = (ax[x : x + 1] * ay).astype(BF16)
        push_rows(cell[2], wt[2], [data[2 * c : 2 * c + 1] for c in range(3)], side_push.at[slot], slice(None), False)

    def side_sum(slot, k):
        dx, dy = SIDES[k]
        first = -REACH if dx < 0 else cells_x - 2
        tile_a = 0 if dy < 0 else cells_y - 8
        for c in range(3):
            if dx:
                total = dot_t(side_wts[slot, 0 : edge * ext_y, :], side_push[slot, c]).reshape(edge, ext_y, cells_z)
                grid[first + REACH : first + REACH + edge, c] += total
            else:
                total = dot_t(side_wts[slot, 0 : inner_x * 16, :], side_push[slot, c]).reshape(inner_x, 2, 8, cells_z)
                grid[2 : 2 + inner_x, c, tile_a : tile_a + 8] += total[:, 0]
                grid[2 : 2 + inner_x, c, cells_y : cells_y + 8] += total[:, 1]

    for pair in (SIDES.index((dx, dy)) for dx, dy in SIDES if dx < 0 or (dx == 0 and dy < 0)):
        other = SIDES.index((-SIDES[pair][0], SIDES[pair][1] if SIDES[pair][0] else -SIDES[pair][1]))

        def both(it, _, pair=pair, other=other):
            side(it, 0, pair)
            side(it, 1, other)
            side_sum(0, pair)
            side_sum(1, other)
            return 0

        lax.fori_loop(0, (jnp.maximum(counts[pair], counts[other]) + 7) // 8 * rounds, both, 0)

    for copy in load_sides:
        copy.wait()
    (x_low, x_high), (y_low, y_high) = (x_sides.at[0], x_sides.at[1]), (y_sides.at[0], y_sides.at[1])

    def add_edges(x, _):
        for c in range(3):
            grid[x, c, 0:cells_y] += x_low[x, c].astype(F32)
            grid[x + REACH + cells_x, c, 0:cells_y] += x_high[x, c].astype(F32)
        return 0

    lax.fori_loop(0, REACH, add_edges, 0)

    def add_sides(x, _):
        for c in range(3):
            pair = jnp.concatenate([y_high[x, c].astype(F32), y_low[x, c].astype(F32)], axis=0)
            grid[x, c, cells_y:ext_y] += pair
        return 0

    lax.fori_loop(0, ext_x, add_sides, 0, unroll=2)

    center_wt = (1.0 - 6.0 * viscosity) / viscosity

    eight = iota((8, cells_z), 0)

    def swept(ref, x, c):
        tiles = [ref[x, c, i : i + 8, :] for i in range(0, ext_y, 8)]
        ups = [pltpu.roll(tile, 1, 0) for tile in tiles]
        downs = [pltpu.roll(tile, 7, 0) for tile in tiles]
        out = []
        for i, tile in enumerate(tiles):
            at = slice(8 * i, 8 * i + 8)
            total = ref[x - 1, c, at, :] + ref[x + 1, c, at, :]
            total = total + jnp.where(eight == 0, ups[i - 1], ups[i])
            total = total + jnp.where(eight == 7, downs[(i + 1) % len(tiles)], downs[i])
            total = total + pltpu.roll(tile, 1, 1) + pltpu.roll(tile, cells_z - 1, 1)
            out.append(center_wt * tile + total)
        return jnp.concatenate(out, axis=0)

    def first_sweep(i, _):
        for x in range(4):
            for c in range(3):
                mid[1 + 4 * i + x, c] = swept(grid, 1 + 4 * i + x, c)
        return 0

    lax.fori_loop(0, (ext_x - 2) // 4, first_sweep, 0)
    for x in range((ext_x - 2) // 4 * 4 + 1, ext_x - 1):
        for c in range(3):
            mid[x, c] = swept(grid, x, c)

    def second_sweep(i, _):
        for j in range(2):
            at_x = 2 + 4 * i + 2 * j
            for c in range(3):
                two = [viscosity * viscosity * swept(mid, at_x + x, c) for x in range(2)]
                grid[at_x, c] = two[0]
                grid[at_x + 1, c] = two[1]
                at = pl.ds(pl.multiple_of((2 * i + j) * 2 * ext_y, 2 * ext_y), 2 * ext_y)
                rounded[c, at, :] = jnp.concatenate(two, axis=0).astype(BF16)
        return 0

    lax.fori_loop(0, inner_x // 4, second_sweep, 0)
    store = pltpu.make_async_copy(grid.at[REACH : REACH + cells_x, :, 0:cells_y, :], field, sems.at[1])
    store.start()

    values[3:8, :] = jnp.zeros((5, points), F32)
    for base in range(0, points, block):
        if blocks > 1:
            build_own(base)
        for c in range(3):
            mixed = lax.dot_general(rounded[c], wts[...], (((0,), (0,)), ((), ())), preferred_element_type=F32)
            values[c : c + 1, base : base + block] = jnp.sum(mixed * depth[...], axis=0, keepdims=True)
    for s in range(sources):
        back[s] = piece_at(lambda i: values[:, i * LANES : (i + 1) * LANES], s * per_peer, per_peer, 0)
    store.wait()


def edge_kernel_x(stored, out_first, out_last, held, sems):
    cells_x = stored.shape[0]
    copies = []
    for i, at in enumerate((0, cells_x - REACH)):
        copies.append(pltpu.make_async_copy(stored.at[at : at + REACH], held.at[i], sems.at[i]))
        copies[-1].start()
    for i, out in enumerate((out_first, out_last)):
        copies[i].wait()
        out[...] = held[i].astype(BF16)


def edge_kernel_y(stored, x_low, x_high, out_first, out_last, held, sides, sems):
    cells_x, cells_y = stored.shape[0], stored.shape[2]
    copies = []
    for i, at in enumerate((0, cells_y - 8)):
        copies.append(pltpu.make_async_copy(stored.at[:, :, at : at + 8, :], held.at[i], sems.at[i]))
    for i, ref in enumerate((x_low, x_high)):
        copies.append(pltpu.make_async_copy(ref, sides.at[i], sems.at[2 + i]))
    for copy in copies:
        copy.start()
    for copy in copies:
        copy.wait()
    out_first[REACH : REACH + cells_x] = held[0, :, :, 0:REACH].astype(BF16)
    out_last[REACH : REACH + cells_x] = held[1, :, :, 8 - REACH :].astype(BF16)
    for i, at in enumerate((0, REACH + cells_x)):
        out_first[at : at + REACH] = sides[i, :, :, 0:8].astype(F32)[:, :, 0:REACH].astype(BF16)
        out_last[at : at + REACH] = sides[i, :, :, cells_y - 8 :].astype(F32)[:, :, 8 - REACH :].astype(BF16)


def last_kernel(per_peer, counts, got, out):
    for m in range(out.shape[1] // LANES):
        acc = jnp.zeros((8, LANES), F32)
        for s in range(m * LANES // per_peer, -(-(m + 1) * LANES // per_peer)):
            at = s * per_peer - m * LANES
            lane = iota((8, LANES), 1)
            ok = (lane >= max(at, 0)) & (lane < jnp.minimum(at + counts[s], min(at + per_peer, LANES)))
            value = got[s]
            value = pltpu.roll(value, at % LANES, 1) if at % LANES else value
            acc = jnp.where(ok, value, acc)
        out[:, m * LANES : (m + 1) * LANES] = acc[0:3]


def staged(velocity, fiber_loads, fractions, corners, neighbours, counts):
    groups_x = lax.axis_size("gx")
    groups_y = lax.axis_size("gy")
    devices = groups_x * groups_y
    slots = fiber_loads.shape[1]
    per_peer = slots // devices
    cells_x, cells_y, cells_z = (velocity.shape[0], velocity.shape[1], velocity.shape[3])
    dims = (groups_x, groups_y, cells_x, cells_y, cells_z, per_peer)
    both = ("gx", "gy")
    width = -(-len(SIDES) * per_peer // LANES) * LANES
    vmem = pl.BlockSpec(memory_space=pltpu.VMEM)
    smem = pl.BlockSpec(memory_space=pltpu.SMEM)
    hbm = pl.BlockSpec(memory_space=pltpu.HBM)

    stored = jnp.transpose(velocity, (0, 2, 1, 3))

    def shifted(first, last, axis):
        peers = lax.axis_size(axis)
        up = [(i, (i + 1) % peers) for i in range(peers)]
        down = [(j, i) for i, j in up]
        return lax.ppermute(last, axis, up), lax.ppermute(first, axis, down)

    slab = (REACH, 3, cells_y, cells_z)
    x_first, x_last = pl.pallas_call(
        edge_kernel_x,
        out_shape=(jax.ShapeDtypeStruct(slab, BF16),) * 2,
        in_specs=[hbm],
        out_specs=(vmem,) * 2,
        scratch_shapes=[pltpu.VMEM((2,) + slab, F32), pltpu.SemaphoreType.DMA((2,))],
        compiler_params=pltpu.CompilerParams(vmem_limit_bytes=61 * MIB),
        name="edges_x",
    )(stored)
    x_low, x_high = shifted(x_first, x_last, "gx")
    payload = pl.pallas_call(
        functools.partial(front_kernel, dims),
        out_shape=jax.ShapeDtypeStruct((devices, 8, width), F32),
        in_specs=[smem] + [vmem] * 4,
        out_specs=vmem,
        scratch_shapes=[
            pltpu.VMEM((8, slots), F32),
            pltpu.VMEM((devices, 8, LANES), F32),
            pltpu.VMEM((8 * devices, LANES), F32),
            pltpu.VMEM((devices, 8, LANES), jnp.int32),
        ],
        compiler_params=pltpu.CompilerParams(vmem_limit_bytes=61 * MIB),
        name="points_out",
    )(counts, fiber_loads, fractions, corners, neighbours)
    received = lax.all_to_all(payload, both, split_axis=0, concat_axis=0, tiled=True)
    strip = (cells_x + 2 * REACH, 3, REACH, cells_z)
    y_first, y_last = pl.pallas_call(
        edge_kernel_y,
        out_shape=(jax.ShapeDtypeStruct(strip, BF16),) * 2,
        in_specs=[hbm] * 3,
        out_specs=(vmem,) * 2,
        scratch_shapes=[
            pltpu.VMEM((2, cells_x, 3, 8, cells_z), F32),
            pltpu.VMEM((2,) + slab, BF16),
            pltpu.SemaphoreType.DMA((4,)),
        ],
        compiler_params=pltpu.CompilerParams(vmem_limit_bytes=61 * MIB),
        name="edges_y",
    )(stored, x_low, x_high)
    y_low, y_high = shifted(y_first, y_last, "gy")

    block = min(slots, 1536)
    ext_x, ext_y, inner_x = cells_x + 2 * REACH, cells_y + 2 * REACH, cells_x + REACH
    side_rows = max((REACH + 2) * ext_y, inner_x * 16)
    field, back = pl.pallas_call(
        functools.partial(main_kernel, dims),
        out_shape=(
            jax.ShapeDtypeStruct(stored.shape, F32),
            jax.ShapeDtypeStruct((devices, 8, LANES), F32),
        ),
        in_specs=[vmem] + [hbm] * 5,
        out_specs=(hbm, vmem),
        scratch_shapes=[
            pltpu.VMEM((8, slots), F32),
            pltpu.VMEM((8, slots), F32),
            pltpu.VMEM((8, slots), F32),
            pltpu.VMEM((8, slots), F32),
            pltpu.VMEM((inner_x * ext_y, block), BF16),
            pltpu.VMEM((3, cells_z, block), BF16),
            pltpu.VMEM((cells_z, block), F32),
            pltpu.VMEM((2, side_rows, 256), BF16),
            pltpu.VMEM((2, 3, cells_z, 256), BF16),
            pltpu.VMEM((ext_x, 3, ext_y, cells_z), F32),
            pltpu.VMEM((ext_x, 3, ext_y, cells_z), F32),
            pltpu.VMEM((3, inner_x * ext_y, cells_z), BF16),
            pltpu.VMEM(stored.shape, F32),
            pltpu.VMEM((8, slots), F32),
            pltpu.VMEM((2,) + slab, BF16),
            pltpu.VMEM((2,) + strip, BF16),
            pltpu.SemaphoreType.DMA((6,)),
        ],
        compiler_params=pltpu.CompilerParams(vmem_limit_bytes=STEP_MIB * MIB),
        name="step",
    )(received, stored, x_low, x_high, y_low, y_high)
    returned = lax.all_to_all(back, both, split_axis=0, concat_axis=0, tiled=True)
    sampled = pl.pallas_call(
        functools.partial(last_kernel, per_peer),
        out_shape=jax.ShapeDtypeStruct((3, slots), F32),
        in_specs=[smem, vmem],
        out_specs=vmem,
        compiler_params=pltpu.CompilerParams(vmem_limit_bytes=12 * MIB),
        name="points_back",
    )(counts, returned)
    return (jnp.transpose(field, (0, 2, 1, 3)), sampled)


def solution(mesh):
    return jax.shard_map(
        staged,
        mesh=mesh,
        in_specs=(
            P("gx", "gy", None, None),
            P(None, ("gx", "gy")),
            P(None, ("gx", "gy")),
            P(None, ("gx", "gy")),
            P(("gx", "gy")),
            P(("gx", "gy")),
        ),
        out_specs=(P("gx", "gy", None, None), P(None, ("gx", "gy"))),
        check_vma=False,
    )
```

time: 97.1 us -> 82.1 us (0.85)
  Pallas kernels: 48 us -> 33.3 us
  other arithmetic: 2.49 us -> 0 us
  blocking collectives: 12.4 us -> 14.4 us
    pallas_call x3 -> x5, Pallas kernels: 48 us -> 33.3 us  [the longest x1 23 us: staged(): pl.pallas_call(functools.partial(main_kernel, dims), out_shape=(jax.Shape...]
    unnamed x0 -> x12, local copies, waits for them, and re-layouts: none -> 2.22 us
    another operation x1 -> x0, other arithmetic: 2.13 us -> none
    all_to_all x1, blocking collectives: 12.4 us -> 14.4 us  [staged(): lax.all_to_all(back, both, split_axis=0, concat_axis=0, tiled=True)]
    reshape x1 -> x0, local copies, waits for them, and re-layouts: 1.29 us -> none  [body(): neighbours.reshape(1, slots)]
  transfers between devices with their start and end apart: 5 -> 5, of which waited for: 4 -> 3; matrix products, arithmetic and copies ran while one was open for 3% -> 0% of each run, Pallas kernels for 0% -> 5%
where the time goes in v2:
time: 82.1 us; the launch traced here: 81.7 us
  Pallas kernels  33.3 us (41%)
  waiting for transfers between devices  17.2 us (21%)
  blocking collectives  14.4 us (18%)
  starting transfers between devices  13.9 us (17%)
  local copies, waits for them, and re-layouts  2.22 us (3%)
    pallas_call x1, Pallas kernels, staged(): pl.pallas_call(functools.partial(main_kernel, dims), out_shape=(jax.Shape...  23 us
    ppermute x4, waiting for transfers between devices, shifted(): return (lax.ppermute(last, axis, up), lax.ppermute(first, axis, down))  17.2 us
    all_to_all x1, blocking collectives, staged(): lax.all_to_all(back, both, split_axis=0, concat_axis=0, tiled=True)  14.4 us
    all_to_all x1, starting transfers between devices, staged(): lax.all_to_all(payload, both, split_axis=0, concat_axis=0, tiled=True)  7.33 us
    ppermute x4, starting transfers between devices, shifted(): return (lax.ppermute(last, axis, up), lax.ppermute(first, axis, down))  6.57 us
    pallas_call x1, Pallas kernels, staged(): pl.pallas_call(functools.partial(front_kernel, dims), out_shape=jax.Shape...  4.77 us
    pallas_call x1, Pallas kernels, staged(): pl.pallas_call(edge_kernel_y, out_shape=(jax.ShapeDtypeStruct(strip, BF16...  2.43 us
    unnamed x12, local copies, waits for them, and re-layouts  2.22 us
  transfers between devices with their start and end apart: 5, of which 3 were waited for; matrix products, arithmetic and copies ran while one was open for 0% of the time, Pallas kernels for 5%

profile of v2, /device:TPU:0, one launch (start us, length us, event | category | flops | bytes accessed | tf_op | source)
XLA Modules:
  0.0 81.7 jit_solution(8662617196477223464)
XLA Ops:
  0.6 4.8 %points_out.1 = f32[32,8,384]{2,1,0:T(8,128)} custom-call(s32[32]{0:T(128)} %counts.3, f32[3,1536]{1,0:T(4,128)} %loads.1, f32[3,1536]{1,0:T(4,128)} %fractions.1, s32[3,1536]{1,0:T(4,128)} %corners.1, s32[1536]{0:T(1024)} %neighbours.1), custom_call_target="tpu_custom_call" | custom-call | tf_op jit(solution)/shard_map/points_out/pallas_call | solution.py:498
  5.4 7.3 %all-to-all-start = ((f32[32,8,384]{2,1,0:T(8,128)}), f32[32,8,384]{2,1,0:T(8,128)S(1)}, u32[]{:S(2)}, u32[]{:S(2)}) async-start(f32[32,8,384]{2,1,0:T(8,128)} %points_out.1), calls=%async_computation | async-start | bytes 786432 | tf_op jit(solution)/shard_map/all_to_all | solution.py:512
  12.7 1.9 %edges_x.1 = (bf16[4,3,32,256]{3,2,1,0:T(8,128)(2,1)}, bf16[4,3,32,256]{3,2,1,0:T(8,128)(2,1)}) custom-call(f32[32,3,32,256]{3,2,1,0:T(8,128)} %bitcast.2), custom_call_target="tpu_custom_call" | custom-call | tf_op jit(solution)/shard_map/edges_x/pallas_call | solution.py:488
  14.6 1.8 %collective-permute-start = (bf16[4,3,32,256]{3,2,1,0:T(8,128)(2,1)}, bf16[4,3,32,256]{3,2,1,0:T(8,128)(2,1)S(1)}, u32[]{:S(2)}, u32[]{:S(2)}) collective-permute-start(bf16[4,3,32,256]{3,2,1,0:T(8,128)(2,1)} %get-tuple-element.8), channel_id=1, source_target_pairs={{0,8},{8,16},{16,24},{24,0},{1,9},{9,17},{17,25},{25,1},{2,10},{10... | collective-permute-start | bytes 589832 | tf_op jit(solution)/shard_map/ppermute | solution.py:485
  16.4 2.1 %collective-permute-start.1 = (bf16[4,3,32,256]{3,2,1,0:T(8,128)(2,1)}, bf16[4,3,32,256]{3,2,1,0:T(8,128)(2,1)S(1)}, u32[]{:S(2)}, u32[]{:S(2)}) collective-permute-start(bf16[4,3,32,256]{3,2,1,0:T(8,128)(2,1)} %get-tuple-element.9), channel_id=1, source_target_pairs={{8,0},{16,8},{24,16},{0,24},{9,1},{17,9},{25,17},{1,25},{10,2},{18... | collective-permute-start | bytes 589832 | tf_op jit(solution)/shard_map/ppermute | solution.py:485
  18.5 10.0 %collective-permute-done.x_low.x_low_in = bf16[4,3,32,256]{3,2,1,0:T(8,128)(2,1)S(1)} collective-permute-done((bf16[4,3,32,256]{3,2,1,0:T(8,128)(2,1)}, bf16[4,3,32,256]{3,2,1,0:T(8,128)(2,1)S(1)}, u32[]{:S(2)}, u32[]{:S(2)}) %collective-permute-start) | collective-permute-done | bytes 196640 | tf_op jit(solution)/shard_map/ppermute | solution.py:485
  28.5 0.0 copy-start.2
  28.5 2.1 %collective-permute-done.1.x_high.x_high_in = bf16[4,3,32,256]{3,2,1,0:T(8,128)(2,1)S(1)} collective-permute-done((bf16[4,3,32,256]{3,2,1,0:T(8,128)(2,1)}, bf16[4,3,32,256]{3,2,1,0:T(8,128)(2,1)S(1)}, u32[]{:S(2)}, u32[]{:S(2)}) %collective-permute-start.1) | collective-permute-done | bytes 196640 | tf_op jit(solution)/shard_map/ppermute | solution.py:485
  30.6 0.0 copy-done.2
  30.6 0.0 copy-start.3
  30.6 0.7 copy-done.3
  31.3 2.4 %edges_y.1 = (bf16[40,3,4,256]{3,2,1,0:T(4,128)(2,1)}, bf16[40,3,4,256]{3,2,1,0:T(4,128)(2,1)}) custom-call(f32[32,3,32,256]{3,2,1,0:T(8,128)} %bitcast.3, bf16[4,3,32,256]{3,2,1,0:T(8,128)(2,1)} %copy-done.2, bf16[4,3,32,256]{3,2,1,0:T(8,128)(2,1)} %copy-done.3), custom_call_target="tpu_custom_call" | custom-call | tf_op jit(solution)/shard_map/edges_y/pallas_call | solution.py:514
  33.7 0.0 copy-start
  33.8 0.1 collective-permute-start.2
  33.8 2.6 %collective-permute-start.3 = (bf16[40,3,4,256]{3,2,1,0:T(4,128)(2,1)}, bf16[40,3,4,256]{3,2,1,0:T(4,128)(2,1)S(1)}, u32[]{:S(2)}, u32[]{:S(2)}) collective-permute-start(bf16[40,3,4,256]{3,2,1,0:T(4,128)(2,1)} %get-tuple-element.11), channel_id=1, source_target_pairs={{1,0},{2,1},{3,2},{4,3},{5,4},{6,5},{7,6},{0,7},{9,8},{10,9},{11,1... | collective-permute-start | bytes 737288 | tf_op jit(solution)/shard_map/ppermute | solution.py:485
  36.5 5.1 %collective-permute-done.2.y_low_in = bf16[40,3,4,256]{3,2,1,0:T(4,128)(2,1)S(1)} collective-permute-done((bf16[40,3,4,256]{3,2,1,0:T(4,128)(2,1)}, bf16[40,3,4,256]{3,2,1,0:T(4,128)(2,1)S(1)}, u32[]{:S(2)}, u32[]{:S(2)}) %collective-permute-start.2) | collective-permute-done | bytes 245792 | tf_op jit(solution)/shard_map/ppermute | solution.py:485
  41.5 0.0 copy-start.4
  41.5 0.0 collective-permute-done.3.y_high_in
  41.5 0.0 copy-start.5
  41.5 0.0 all-to-all-done.got
  41.5 0.7 copy-done.4
  42.2 0.1 copy-done.5
  42.3 0.0 copy-start.1
  42.3 0.7 copy-done.1
  43.0 23.0 %step.1 = (f32[32,3,32,256]{3,2,1,0:T(8,128)}, f32[32,8,128]{2,1,0:T(8,128)}) custom-call(f32[32,8,384]{2,1,0:T(8,128)} %copy-done.1, f32[32,3,32,256]{3,2,1,0:T(8,128)} %bitcast.4, bf16[4,3,32,256]{3,2,1,0:T(8,128)(2,1)} %copy-done.2, bf16[4,3,32,256]{3,2,1,0:T(8,128)(2,1)} %copy-done.3, bf16[40,3,4,256]{3,2,1,0:T(4,128)(2,1)} %copy-done.4, ...), custom_call_target="tpu_custom_call" | custom-call | tf_op jit(solution)/shard_map/step/pallas_call | solution.py:532
  66.0 14.4 %all_to_all.10.got = f32[32,8,128]{2,1,0:T(8,128)S(1)} all-to-all(f32[32,8,128]{2,1,0:T(8,128)} %get-tuple-element.13), channel_id=1, replica_groups=mesh['gx'=4,'gy'=8] {'gx','gy'}, dimensions={0} | all-to-all | bytes 262144 | tf_op jit(solution)/shard_map/all_to_all | solution.py:562
  80.4 0.0 copy-done
  80.4 1.3 %points_back.1 = f32[3,1536]{1,0:T(4,128)} custom-call(s32[32]{0:T(128)S(1)} %copy-done, f32[32,8,128]{2,1,0:T(8,128)S(1)} %all_to_all.10.got), custom_call_target="tpu_custom_call" | custom-call | tf_op jit(solution)/shard_map/points_back/pallas_call | solution.py:563
Async XLA Ops:
  5.4 36.1 %all-to-all-start = ((f32[32,8,384]{2,1,0:T(8,128)}), f32[32,8,384]{2,1,0:T(8,128)S(1)}, u32[]{:S(2)}, u32[]{:S(2)}) async-start(f32[32,8,384]{2,1,0:T(8,128)} %points_out.1), calls=%async_computation | async-start | bytes 786432 | tf_op jit(solution)/shard_map/all_to_all | solution.py:512
  14.6 13.9 %collective-permute-start = (bf16[4,3,32,256]{3,2,1,0:T(8,128)(2,1)}, bf16[4,3,32,256]{3,2,1,0:T(8,128)(2,1)S(1)}, u32[]{:S(2)}, u32[]{:S(2)}) collective-permute-start(bf16[4,3,32,256]{3,2,1,0:T(8,128)(2,1)} %get-tuple-element.8), channel_id=1, source_target_pairs={{0,8},{8,16},{16,24},{24,0},{1,9},{9,17},{17,25},{25,1},{2,10},{10... | collective-permute-start | bytes 589832 | tf_op jit(solution)/shard_map/ppermute | solution.py:485
  16.4 14.2 %collective-permute-start.1 = (bf16[4,3,32,256]{3,2,1,0:T(8,128)(2,1)}, bf16[4,3,32,256]{3,2,1,0:T(8,128)(2,1)S(1)}, u32[]{:S(2)}, u32[]{:S(2)}) collective-permute-start(bf16[4,3,32,256]{3,2,1,0:T(8,128)(2,1)} %get-tuple-element.9), channel_id=1, source_target_pairs={{8,0},{16,8},{24,16},{0,24},{9,1},{17,9},{25,17},{1,25},{10,2},{18... | collective-permute-start | bytes 589832 | tf_op jit(solution)/shard_map/ppermute | solution.py:485
  28.5 2.1 %copy-start.2 = (bf16[4,3,32,256]{3,2,1,0:T(8,128)(2,1)}, bf16[4,3,32,256]{3,2,1,0:T(8,128)(2,1)S(1)}, u32[]{:S(2)}) copy-start(bf16[4,3,32,256]{3,2,1,0:T(8,128)(2,1)S(1)} %collective-permute-done.x_low.x_low_in) | copy-start | bytes 589828
  30.6 0.7 copy-start.3
  33.7 46.7 %copy-start = (s32[32]{0:T(128)S(1)}, s32[32]{0:T(128)}, u32[]{:S(2)}) copy-start(s32[32]{0:T(128)} %counts.3) | copy-start | bytes 388
  33.8 7.8 %collective-permute-start.2 = (bf16[40,3,4,256]{3,2,1,0:T(4,128)(2,1)}, bf16[40,3,4,256]{3,2,1,0:T(4,128)(2,1)S(1)}, u32[]{:S(2)}, u32[]{:S(2)}) collective-permute-start(bf16[40,3,4,256]{3,2,1,0:T(4,128)(2,1)} %get-tuple-element.10), channel_id=1, source_target_pairs={{0,1},{1,2},{2,3},{3,4},{4,5},{5,6},{6,7},{7,0},{8,9},{9,10},{10,1... | collective-permute-start | bytes 737288 | tf_op jit(solution)/shard_map/ppermute | solution.py:485
  33.8 7.7 %collective-permute-start.3 = (bf16[40,3,4,256]{3,2,1,0:T(4,128)(2,1)}, bf16[40,3,4,256]{3,2,1,0:T(4,128)(2,1)S(1)}, u32[]{:S(2)}, u32[]{:S(2)}) collective-permute-start(bf16[40,3,4,256]{3,2,1,0:T(4,128)(2,1)} %get-tuple-element.11), channel_id=1, source_target_pairs={{1,0},{2,1},{3,2},{4,3},{5,4},{6,5},{7,6},{0,7},{9,8},{10,9},{11,1... | collective-permute-start | bytes 737288 | tf_op jit(solution)/shard_map/ppermute | solution.py:485
  41.5 0.7 copy-start.4
  41.5 0.8 copy-start.5
  42.3 0.7 copy-start.1

commit v3 on v2

--- a/solution.py
+++ b/solution.py
@@ -258,24 +258,6 @@
     def dot_t(a, b):
         return lax.dot_general(a, b, (((1,), (1,)), ((), ())), preferred_element_type=F32)
 
-    for base in range(0, points, block):
-        build_own(base)
-        if base == 0:
-            load_vel.wait()
-
-        def spread_own(c, _, base=base):
-            total = dot_t(wts[...], push[c]).reshape(inner_x, ext_y, cells_z)
-            if base == 0:
-                grid[2 : 2 + inner_x, c] = total
-                grid[0:2, c] = jnp.zeros((2, ext_y, cells_z), F32)
-                grid[2 + inner_x :, c] = jnp.zeros((2, ext_y, cells_z), F32)
-                grid[REACH : REACH + cells_x, c, 0:cells_y] = total[2 : 2 + cells_x, 0:cells_y] + own_vel[:, c]
-            else:
-                grid[2 : 2 + inner_x, c] += total
-            return 0
-
-        lax.fori_loop(0, 3, spread_own, 0)
-
     edge = REACH + 2
     together = chunk // 8
     rounds = sources // together
@@ -286,10 +268,8 @@
         jnp.max(jnp.where((sub == 7) & (lane == LANES - 8 + k), most, 0.0)).astype(jnp.int32) for k in range(len(SIDES))
     ]
 
-    def side(it, slot, k):
-        dx, dy = SIDES[k]
+    def side(it, slot, k, dx, dy):
         first = -REACH if dx < 0 else cells_x - 2
-        tile_a = 0 if dy < 0 else cells_y - 8
         start = k * per_peer + (it // rounds if rounds > 1 else it) * 8
         source = (it % rounds if rounds > 1 else 0) * together
         at = pl.ds(pl.multiple_of(start // LANES * LANES, LANES), LANES)
@@ -305,7 +285,7 @@
         floor, sine, cosine = split(data)
         cell = [floor[2 * c + 1 : 2 * c + 2] for c in range(3)]
         cell[0] = cell[0] + float(dx * cells_x)
-        cell[1] = cell[1] + float(dy * cells_y)
+        cell[1] = cell[1] + jnp.asarray(dy * cells_y).astype(F32)
         wt = [weights(sine[2 * c + 1 : 2 * c + 2], cosine[2 * c + 1 : 2 * c + 2]) for c in range(3)]
         if dx:
             ax = along(cell[0], wt[0], 8, lambda r: r + first)
@@ -313,6 +293,7 @@
             for x in range(0, edge, 2):
                 side_wts[slot, x * ext_y : (x + 2) * ext_y, :] = pair_rows(ax, ay, x)
         else:
+            tile_a = 0 if dy < 0 else cells_y - 8
             ax = along(cell[0], wt[0], -(-inner_x // 8) * 8, lambda r: r - 2)
             ay = along(cell[1], wt[1], 16, lambda r: circle(jnp.where(r < 8, r + tile_a, r - 8 + cells_y)))
             for x in range(inner_x):
@@ -332,17 +313,44 @@
                 grid[2 : 2 + inner_x, c, tile_a : tile_a + 8] += total[:, 0]
                 grid[2 : 2 + inner_x, c, cells_y : cells_y + 8] += total[:, 1]
 
-    for pair in (SIDES.index((dx, dy)) for dx, dy in SIDES if dx < 0 or (dx == 0 and dy < 0)):
-        other = SIDES.index((-SIDES[pair][0], SIDES[pair][1] if SIDES[pair][0] else -SIDES[pair][1]))
-
-        def both(it, _, pair=pair, other=other):
-            side(it, 0, pair)
-            side(it, 1, other)
-            side_sum(0, pair)
-            side_sum(1, other)
+    for base in range(0, points, block):
+        build_own(base)
+        if base == 0:
+            load_vel.wait()
+
+        def spread_own(c, _, base=base):
+            if base == 0:
+                side(0, 2 * c, c, -1, c - 1)
+                side(0, 2 * c + 1, c + 3, 1, c - 1)
+            total = dot_t(wts[...], push[c]).reshape(inner_x, ext_y, cells_z)
+            if base == 0:
+                grid[2 : 2 + inner_x, c] = total
+                grid[0:2, c] = jnp.zeros((2, ext_y, cells_z), F32)
+                grid[2 + inner_x :, c] = jnp.zeros((2, ext_y, cells_z), F32)
+                grid[REACH : REACH + cells_x, c, 0:cells_y] = total[2 : 2 + cells_x, 0:cells_y] + own_vel[:, c]
+            else:
+                grid[2 : 2 + inner_x, c] += total
             return 0
 
-        lax.fori_loop(0, (jnp.maximum(counts[pair], counts[other]) + 7) // 8 * rounds, both, 0)
+        lax.fori_loop(0, 3, spread_own, 0)
+
+    pairs = ((0, 3), (1, 4), (2, 5), (6, 7))
+    side(0, 6, 6, 0, -1)
+    side(0, 7, 7, 0, 1)
+    for i, pair in enumerate(pairs):
+        for j, k in enumerate(pair):
+            side_sum(2 * i + j, k)
+    for pair in pairs:
+
+        def both(it, _, pair=pair):
+            for j, k in enumerate(pair):
+                side(it, j, k, *SIDES[k])
+            for j, k in enumerate(pair):
+                side_sum(j, k)
+            return 0
+
+        most_of = jnp.maximum(counts[pair[0]], counts[pair[1]])
+        lax.fori_loop(1, (most_of + 7) // 8 * rounds, both, 0)
 
     for copy in load_sides:
         copy.wait()
@@ -416,7 +424,7 @@
             mixed = lax.dot_general(rounded[c], wts[...], (((0,), (0,)), ((), ())), preferred_element_type=F32)
             values[c : c + 1, base : base + block] = jnp.sum(mixed * depth[...], axis=0, keepdims=True)
     for s in range(sources):
-        back[s] = piece_at(lambda i: values[:, i * LANES : (i + 1) * LANES], s * per_peer, per_peer, 0)
+        back[s] = piece_at(lambda i: values[:, i * LANES : (i + 1) * LANES], s * per_peer, per_peer, 0)[0:4]
     store.wait()
 
 
@@ -451,10 +459,10 @@
 
 def last_kernel(per_peer, counts, got, out):
     for m in range(out.shape[1] // LANES):
-        acc = jnp.zeros((8, LANES), F32)
+        acc = jnp.zeros((4, LANES), F32)
         for s in range(m * LANES // per_peer, -(-(m + 1) * LANES // per_peer)):
             at = s * per_peer - m * LANES
-            lane = iota((8, LANES), 1)
+            lane = iota((4, LANES), 1)
             ok = (lane >= max(at, 0)) & (lane < jnp.minimum(at + counts[s], min(at + per_peer, LANES)))
             value = got[s]
             value = pltpu.roll(value, at % LANES, 1) if at % LANES else value
@@ -533,7 +541,7 @@
         functools.partial(main_kernel, dims),
         out_shape=(
             jax.ShapeDtypeStruct(stored.shape, F32),
-            jax.ShapeDtypeStruct((devices, 8, LANES), F32),
+            jax.ShapeDtypeStruct((devices, 4, LANES), F32),
         ),
         in_specs=[vmem] + [hbm] * 5,
         out_specs=(hbm, vmem),
@@ -545,8 +553,8 @@
             pltpu.VMEM((inner_x * ext_y, block), BF16),
             pltpu.VMEM((3, cells_z, block), BF16),
             pltpu.VMEM((cells_z, block), F32),
-            pltpu.VMEM((2, side_rows, 256), BF16),
-            pltpu.VMEM((2, 3, cells_z, 256), BF16),
+            pltpu.VMEM((8, side_rows, 256), BF16),
+            pltpu.VMEM((8, 3, cells_z, 256), BF16),
             pltpu.VMEM((ext_x, 3, ext_y, cells_z), F32),
             pltpu.VMEM((ext_x, 3, ext_y, cells_z), F32),
             pltpu.VMEM((3, inner_x * ext_y, cells_z), BF16),

time: 82.1 us -> 80.5 us (0.981)
  no operation moved by 1% of the time
where the time goes in v3:
time: 80.5 us; the launch traced here: 80.2 us
  Pallas kernels  32.5 us (40%)
  waiting for transfers between devices  17.2 us (21%)
  starting transfers between devices  13.9 us (17%)
  blocking collectives  13.6 us (17%)
  local copies, waits for them, and re-layouts  2.22 us (3%)
    pallas_call x1, Pallas kernels, staged(): pl.pallas_call(functools.partial(main_kernel, dims), out_shape=(jax.Shape...  22.2 us
    ppermute x4, waiting for transfers between devices, shifted(): return (lax.ppermute(last, axis, up), lax.ppermute(first, axis, down))  17.2 us
    all_to_all x1, blocking collectives, staged(): lax.all_to_all(back, both, split_axis=0, concat_axis=0, tiled=True)  13.6 us
    all_to_all x1, starting transfers between devices, staged(): lax.all_to_all(payload, both, split_axis=0, concat_axis=0, tiled=True)  7.33 us
    ppermute x4, starting transfers between devices, shifted(): return (lax.ppermute(last, axis, up), lax.ppermute(first, axis, down))  6.57 us
    pallas_call x1, Pallas kernels, staged(): pl.pallas_call(functools.partial(front_kernel, dims), out_shape=jax.Shape...  4.77 us
    pallas_call x1, Pallas kernels, staged(): pl.pallas_call(edge_kernel_y, out_shape=(jax.ShapeDtypeStruct(strip, BF16...  2.43 us
    unnamed x12, local copies, waits for them, and re-layouts  2.22 us
  transfers between devices with their start and end apart: 5, of which 3 were waited for; matrix products, arithmetic and copies ran while one was open for 0% of the time, Pallas kernels for 5%

profile of v3, /device:TPU:0, one launch (start us, length us, event | category | flops | bytes accessed | tf_op | source)
XLA Modules:
  0.0 80.2 jit_solution(9777746673351537111)
XLA Ops:
  0.6 4.8 %points_out.1 = f32[32,8,384]{2,1,0:T(8,128)} custom-call(s32[32]{0:T(128)} %counts.3, f32[3,1536]{1,0:T(4,128)} %loads.1, f32[3,1536]{1,0:T(4,128)} %fractions.1, s32[3,1536]{1,0:T(4,128)} %corners.1, s32[1536]{0:T(1024)} %neighbours.1), custom_call_target="tpu_custom_call" | custom-call | tf_op jit(solution)/shard_map/points_out/pallas_call | solution.py:506
  5.4 7.3 %all-to-all-start = ((f32[32,8,384]{2,1,0:T(8,128)}), f32[32,8,384]{2,1,0:T(8,128)S(1)}, u32[]{:S(2)}, u32[]{:S(2)}) async-start(f32[32,8,384]{2,1,0:T(8,128)} %points_out.1), calls=%async_computation | async-start | bytes 786432 | tf_op jit(solution)/shard_map/all_to_all | solution.py:520
  12.7 1.9 %edges_x.1 = (bf16[4,3,32,256]{3,2,1,0:T(8,128)(2,1)}, bf16[4,3,32,256]{3,2,1,0:T(8,128)(2,1)}) custom-call(f32[32,3,32,256]{3,2,1,0:T(8,128)} %bitcast.2), custom_call_target="tpu_custom_call" | custom-call | tf_op jit(solution)/shard_map/edges_x/pallas_call | solution.py:496
  14.6 1.8 %collective-permute-start = (bf16[4,3,32,256]{3,2,1,0:T(8,128)(2,1)}, bf16[4,3,32,256]{3,2,1,0:T(8,128)(2,1)S(1)}, u32[]{:S(2)}, u32[]{:S(2)}) collective-permute-start(bf16[4,3,32,256]{3,2,1,0:T(8,128)(2,1)} %get-tuple-element.8), channel_id=1, source_target_pairs={{0,8},{8,16},{16,24},{24,0},{1,9},{9,17},{17,25},{25,1},{2,10},{10... | collective-permute-start | bytes 589832 | tf_op jit(solution)/shard_map/ppermute | solution.py:493
  16.4 2.1 %collective-permute-start.1 = (bf16[4,3,32,256]{3,2,1,0:T(8,128)(2,1)}, bf16[4,3,32,256]{3,2,1,0:T(8,128)(2,1)S(1)}, u32[]{:S(2)}, u32[]{:S(2)}) collective-permute-start(bf16[4,3,32,256]{3,2,1,0:T(8,128)(2,1)} %get-tuple-element.9), channel_id=1, source_target_pairs={{8,0},{16,8},{24,16},{0,24},{9,1},{17,9},{25,17},{1,25},{10,2},{18... | collective-permute-start | bytes 589832 | tf_op jit(solution)/shard_map/ppermute | solution.py:493
  18.5 10.0 %collective-permute-done.x_low.x_low_in = bf16[4,3,32,256]{3,2,1,0:T(8,128)(2,1)S(1)} collective-permute-done((bf16[4,3,32,256]{3,2,1,0:T(8,128)(2,1)}, bf16[4,3,32,256]{3,2,1,0:T(8,128)(2,1)S(1)}, u32[]{:S(2)}, u32[]{:S(2)}) %collective-permute-start) | collective-permute-done | bytes 196640 | tf_op jit(solution)/shard_map/ppermute | solution.py:493
  28.5 0.0 copy-start.2
  28.5 2.1 %collective-permute-done.1.x_high.x_high_in = bf16[4,3,32,256]{3,2,1,0:T(8,128)(2,1)S(1)} collective-permute-done((bf16[4,3,32,256]{3,2,1,0:T(8,128)(2,1)}, bf16[4,3,32,256]{3,2,1,0:T(8,128)(2,1)S(1)}, u32[]{:S(2)}, u32[]{:S(2)}) %collective-permute-start.1) | collective-permute-done | bytes 196640 | tf_op jit(solution)/shard_map/ppermute | solution.py:493
  30.6 0.0 copy-done.2
  30.6 0.0 copy-start.3
  30.6 0.7 copy-done.3
  31.3 2.4 %edges_y.1 = (bf16[40,3,4,256]{3,2,1,0:T(4,128)(2,1)}, bf16[40,3,4,256]{3,2,1,0:T(4,128)(2,1)}) custom-call(f32[32,3,32,256]{3,2,1,0:T(8,128)} %bitcast.3, bf16[4,3,32,256]{3,2,1,0:T(8,128)(2,1)} %copy-done.2, bf16[4,3,32,256]{3,2,1,0:T(8,128)(2,1)} %copy-done.3), custom_call_target="tpu_custom_call" | custom-call | tf_op jit(solution)/shard_map/edges_y/pallas_call | solution.py:522
  33.7 0.0 copy-start
  33.8 0.1 collective-permute-start.2
  33.8 2.6 %collective-permute-start.3 = (bf16[40,3,4,256]{3,2,1,0:T(4,128)(2,1)}, bf16[40,3,4,256]{3,2,1,0:T(4,128)(2,1)S(1)}, u32[]{:S(2)}, u32[]{:S(2)}) collective-permute-start(bf16[40,3,4,256]{3,2,1,0:T(4,128)(2,1)} %get-tuple-element.11), channel_id=1, source_target_pairs={{1,0},{2,1},{3,2},{4,3},{5,4},{6,5},{7,6},{0,7},{9,8},{10,9},{11,1... | collective-permute-start | bytes 737288 | tf_op jit(solution)/shard_map/ppermute | solution.py:493
  36.5 5.1 %collective-permute-done.2.y_low_in = bf16[40,3,4,256]{3,2,1,0:T(4,128)(2,1)S(1)} collective-permute-done((bf16[40,3,4,256]{3,2,1,0:T(4,128)(2,1)}, bf16[40,3,4,256]{3,2,1,0:T(4,128)(2,1)S(1)}, u32[]{:S(2)}, u32[]{:S(2)}) %collective-permute-start.2) | collective-permute-done | bytes 245792 | tf_op jit(solution)/shard_map/ppermute | solution.py:493
  41.5 0.0 copy-start.4
  41.5 0.0 collective-permute-done.3.y_high_in
  41.5 0.0 copy-start.5
  41.5 0.0 all-to-all-done.got
  41.5 0.7 copy-done.4
  42.2 0.1 copy-done.5
  42.3 0.0 copy-start.1
  42.3 0.7 copy-done.1
  43.0 22.2 %step.1 = (f32[32,3,32,256]{3,2,1,0:T(8,128)}, f32[32,4,128]{2,1,0:T(4,128)}) custom-call(f32[32,8,384]{2,1,0:T(8,128)} %copy-done.1, f32[32,3,32,256]{3,2,1,0:T(8,128)} %bitcast.4, bf16[4,3,32,256]{3,2,1,0:T(8,128)(2,1)} %copy-done.2, bf16[4,3,32,256]{3,2,1,0:T(8,128)(2,1)} %copy-done.3, bf16[40,3,4,256]{3,2,1,0:T(4,128)(2,1)} %copy-done.4, ...), custom_call_target="tpu_custom_call" | custom-call | tf_op jit(solution)/shard_map/step/pallas_call | solution.py:540
  65.3 13.6 %all_to_all.10.got = f32[32,4,128]{2,1,0:T(4,128)S(1)} all-to-all(f32[32,4,128]{2,1,0:T(4,128)} %get-tuple-element.13), channel_id=1, replica_groups=mesh['gx'=4,'gy'=8] {'gx','gy'}, dimensions={0} | all-to-all | bytes 131072 | tf_op jit(solution)/shard_map/all_to_all | solution.py:570
  78.9 0.0 copy-done
  78.9 1.3 %points_back.1 = f32[3,1536]{1,0:T(4,128)} custom-call(s32[32]{0:T(128)S(1)} %copy-done, f32[32,4,128]{2,1,0:T(4,128)S(1)} %all_to_all.10.got), custom_call_target="tpu_custom_call" | custom-call | tf_op jit(solution)/shard_map/points_back/pallas_call | solution.py:571
Async XLA Ops:
  5.4 36.1 %all-to-all-start = ((f32[32,8,384]{2,1,0:T(8,128)}), f32[32,8,384]{2,1,0:T(8,128)S(1)}, u32[]{:S(2)}, u32[]{:S(2)}) async-start(f32[32,8,384]{2,1,0:T(8,128)} %points_out.1), calls=%async_computation | async-start | bytes 786432 | tf_op jit(solution)/shard_map/all_to_all | solution.py:520
  14.6 13.9 %collective-permute-start = (bf16[4,3,32,256]{3,2,1,0:T(8,128)(2,1)}, bf16[4,3,32,256]{3,2,1,0:T(8,128)(2,1)S(1)}, u32[]{:S(2)}, u32[]{:S(2)}) collective-permute-start(bf16[4,3,32,256]{3,2,1,0:T(8,128)(2,1)} %get-tuple-element.8), channel_id=1, source_target_pairs={{0,8},{8,16},{16,24},{24,0},{1,9},{9,17},{17,25},{25,1},{2,10},{10... | collective-permute-start | bytes 589832 | tf_op jit(solution)/shard_map/ppermute | solution.py:493
  16.4 14.2 %collective-permute-start.1 = (bf16[4,3,32,256]{3,2,1,0:T(8,128)(2,1)}, bf16[4,3,32,256]{3,2,1,0:T(8,128)(2,1)S(1)}, u32[]{:S(2)}, u32[]{:S(2)}) collective-permute-start(bf16[4,3,32,256]{3,2,1,0:T(8,128)(2,1)} %get-tuple-element.9), channel_id=1, source_target_pairs={{8,0},{16,8},{24,16},{0,24},{9,1},{17,9},{25,17},{1,25},{10,2},{18... | collective-permute-start | bytes 589832 | tf_op jit(solution)/shard_map/ppermute | solution.py:493
  28.5 2.1 %copy-start.2 = (bf16[4,3,32,256]{3,2,1,0:T(8,128)(2,1)}, bf16[4,3,32,256]{3,2,1,0:T(8,128)(2,1)S(1)}, u32[]{:S(2)}) copy-start(bf16[4,3,32,256]{3,2,1,0:T(8,128)(2,1)S(1)} %collective-permute-done.x_low.x_low_in) | copy-start | bytes 589828
  30.6 0.7 copy-start.3
  33.7 45.2 %copy-start = (s32[32]{0:T(128)S(1)}, s32[32]{0:T(128)}, u32[]{:S(2)}) copy-start(s32[32]{0:T(128)} %counts.3) | copy-start | bytes 388
  33.8 7.8 %collective-permute-start.2 = (bf16[40,3,4,256]{3,2,1,0:T(4,128)(2,1)}, bf16[40,3,4,256]{3,2,1,0:T(4,128)(2,1)S(1)}, u32[]{:S(2)}, u32[]{:S(2)}) collective-permute-start(bf16[40,3,4,256]{3,2,1,0:T(4,128)(2,1)} %get-tuple-element.10), channel_id=1, source_target_pairs={{0,1},{1,2},{2,3},{3,4},{4,5},{5,6},{6,7},{7,0},{8,9},{9,10},{10,1... | collective-permute-start | bytes 737288 | tf_op jit(solution)/shard_map/ppermute | solution.py:493
  33.8 7.7 %collective-permute-start.3 = (bf16[40,3,4,256]{3,2,1,0:T(4,128)(2,1)}, bf16[40,3,4,256]{3,2,1,0:T(4,128)(2,1)S(1)}, u32[]{:S(2)}, u32[]{:S(2)}) collective-permute-start(bf16[40,3,4,256]{3,2,1,0:T(4,128)(2,1)} %get-tuple-element.11), channel_id=1, source_target_pairs={{1,0},{2,1},{3,2},{4,3},{5,4},{6,5},{7,6},{0,7},{9,8},{10,9},{11,1... | collective-permute-start | bytes 737288 | tf_op jit(solution)/shard_map/ppermute | solution.py:493
  41.5 0.7 copy-start.4
  41.5 0.8 copy-start.5
  42.3 0.7 copy-start.1
